TPU v7x, 256 devices: a whole 4x4x8 slice. The times are simulated.
256 devices in a mesh: dp: 4 (over x), expert: 64 (over z, y, core).
Axes of the slice: x: 4, y: 4, z: 8, core: 2. Of those that a mesh axis runs over, the one named last changes fastest.
Arguments:
- tokens: bfloat16 [32768, 2048], P(('dp', 'expert')), may hold values from -6 to 6
- expert_ids: int32 [32768, 2], P(('dp', 'expert')), may hold values from 0 to 63, all different within a row; in each aligned block of 128 rows (0 to 127, 128 to 255, ...) at most 6 rows name the same one
- gates: bfloat16 [32768, 2], P(('dp', 'expert')), may hold values from 0.049804688 to 1
- cotangent: bfloat16 [32768, 2048], P(('dp', 'expert')), may hold values from -6 to 6
- w_gate: bfloat16 [64, 2048, 768], P('expert'), may hold values from -0.125 to 0.125
- w_up: bfloat16 [64, 2048, 768], P('expert'), may hold values from -0.125 to 0.125
- w_down: bfloat16 [64, 768, 2048], P('expert'), may hold values from -0.21875 to 0.21875
Outputs:
- grad_tokens: bfloat16 [32768, 2048], P(('dp', 'expert'))
- grad_gates: bfloat16 [32768, 2], P(('dp', 'expert'))
- grad_w_gate: bfloat16 [64, 2048, 768], P('expert', 'dp')
- grad_w_up: bfloat16 [64, 2048, 768], P('expert', 'dp')
- grad_w_down: bfloat16 [64, 768, 2048], P('expert', None, 'dp')
Inputs may be any that keep to these rules, and one draw needn't show every extreme that they name: `expert_ids`: within the 128 rows of one device no expert is named by more than 6 rows, and in some of these aligned blocks an expert is named by exactly 6 rows.
All inputs are finite; a program needn't handle non-finite values.
Results may differ from a plain program's by a relative error of at most 0.013.
Values may be sent and summed in bfloat16 or wider, within the bound.
No kernel may reach another device: no remote copies, remote signals or barrier semaphores. Data moves between devices by JAX's collectives and lax.ppermute only.
A program may use at most 128 MiB of HBM per device.

v0:
```python
import functools

import jax
import jax.numpy as jnp
import numpy as np
from jax import lax
from jax.experimental import pallas as pl
from jax.experimental.pallas import tpu as pltpu
from jax.sharding import PartitionSpec as P

BF = jnp.bfloat16
F32 = jnp.float32
PARTS = 4
HINT = 10
LINES = 8
GROUP = 8
LIMIT = 40 * 1024 * 1024
MOST = 60 * 1024 * 1024
SM = pl.BlockSpec(memory_space=pltpu.SMEM)


def dot(a, b):
    return jnp.dot(a, b, preferred_element_type=F32)


def dot_t(a, b):
    return lax.dot_general(a, b, (((1,), (1,)), ((), ())), preferred_element_type=F32)


def t_dot(a, b):
    return lax.dot_general(a, b, (((0,), (0,)), ((), ())), preferred_element_type=F32)


def whole(dims):
    return pl.BlockSpec(dims, lambda *_: (0,) * len(dims))


def call(kernel, outs, args, specs=None, out_specs=None, grid=(1,), scratch=(), flops=0, limit=LIMIT):
    size = sum(int(np.prod(a.shape)) * a.dtype.itemsize for a in list(args) + list(outs))
    return pl.pallas_call(
        kernel,
        out_shape=outs,
        grid=grid,
        in_specs=specs or [whole(a.shape) for a in args],
        out_specs=out_specs or [whole(a.shape) for a in outs],
        scratch_shapes=scratch,
        compiler_params=pltpu.CompilerParams(vmem_limit_bytes=limit),
        cost_estimate=pl.CostEstimate(flops=int(flops), bytes_accessed=size, transcendentals=0),
    )(*args)


def shape(dims, dtype=BF):
    return jax.ShapeDtypeStruct(dims, dtype)


def permutation(cap):
    rows = GROUP * PARTS * cap
    r = np.arange(rows)
    part, owner, slot = r // (GROUP * cap), r // cap % GROUP, r % cap
    mat = np.zeros((rows, rows), np.float32)
    mat[r, owner * PARTS * cap + part * cap + slot] = 1.0
    return mat


def line_permutation(cap):
    rows = GROUP * PARTS * cap
    r = np.arange(rows)
    block, owner, line = r // (GROUP * LINES), r // LINES % GROUP, r % LINES
    part, slot = (block * LINES + line) // cap, (block * LINES + line) % cap
    mat = np.zeros((rows, rows), np.float32)
    mat[r, part * GROUP * cap + owner * cap + slot] = 1.0
    return mat


def route(ids_ref, owners, cap):
    top, toks = ids_ref.shape
    experts = lax.broadcasted_iota(jnp.int32, (owners, toks), 0)
    earlier = jnp.where(
        lax.broadcasted_iota(jnp.int32, (toks, toks), 0) < lax.broadcasted_iota(jnp.int32, (toks, toks), 1), 1.0, 0.0
    ).astype(BF)
    seen = jnp.zeros((owners, 1), F32)
    picks, places, slots = [], [], []
    for k in range(top):
        ids = ids_ref[k : k + 1, :]
        pick = jnp.where(experts == ids, 1.0, 0.0)
        before = dot(pick.astype(BF), earlier) + seen
        seen = seen + jnp.sum(pick, axis=1, keepdims=True)
        place = jnp.sum(pick * before, axis=0, keepdims=True).astype(jnp.int32)
        picks.append(pick)
        places.append(place)
        slots.append(ids * cap + place)
    return picks, places, slots


def hits(slots, slot_count):
    rows = lax.broadcasted_iota(jnp.int32, (slot_count, slots[0].shape[1]), 0)
    return [rows == s for s in slots]


def pack(full_ref, packer_ref, out_ref, cap):
    block = GROUP * cap
    for g in range(full_ref.shape[0] // block):
        tall = tall_rows(full_ref, g, block)
        out_ref[g * block * PARTS : (g + 1) * block * PARTS, :] = t_dot(packer_ref[...], tall).astype(BF)


def unpack(in_ref, packer_ref, full_ref, cap):
    block, wide = GROUP * cap, in_ref.shape[1]
    for g in range(full_ref.shape[0] // block):
        tall = dot(packer_ref[...], in_ref[g * block * PARTS : (g + 1) * block * PARTS, :]).astype(BF)
        for q in range(PARTS):
            full_ref[g * block : (g + 1) * block, q * wide : (q + 1) * wide] = tall[q * block : (q + 1) * block, :]


def tall_rows(full_ref, g, block):
    wide = full_ref.shape[1] // PARTS
    return jnp.concatenate(
        [full_ref[g * block : (g + 1) * block, q * wide : (q + 1) * wide] for q in range(PARTS)], axis=0
    )


def pack_lines(full_ref, liner_ref, out_ref, cap):
    block, wide, high = GROUP * cap, full_ref.shape[1] // PARTS, GROUP * LINES
    for g in range(full_ref.shape[0] // block):
        lined = dot(liner_ref[...], tall_rows(full_ref, g, block)).astype(BF)
        for c in range(lined.shape[0] // high):
            out_ref[g * high : (g + 1) * high, c * wide : (c + 1) * wide] = lined[c * high : (c + 1) * high, :]


def unpack_lines(in_ref, liner_ref, full_ref, cap):
    block, wide, high = GROUP * cap, full_ref.shape[1] // PARTS, GROUP * LINES
    for g in range(full_ref.shape[0] // block):
        lined = jnp.concatenate(
            [in_ref[g * high : (g + 1) * high, c * wide : (c + 1) * wide] for c in range(PARTS * cap // LINES)], axis=0
        )
        tall = t_dot(liner_ref[...], lined).astype(BF)
        for q in range(PARTS):
            full_ref[g * block : (g + 1) * block, q * wide : (q + 1) * wide] = tall[q * block : (q + 1) * block, :]


def send_kernel(owners, cap, scaled, ids_ref, gates_ref, x_ref, packer_ref, out_ref, full_ref):
    _, _, slots = route(ids_ref, owners, cap)
    found = hits(slots, owners * cap)
    pick = jnp.where(functools.reduce(jnp.logical_or, found), 1.0, 0.0).astype(BF)
    full = dot(pick, x_ref[...])
    if scaled:
        weight = sum(
            jnp.where(f, gates_ref[k : k + 1, :].astype(F32), 0.0) for k, f in enumerate(found)
        )
        full = jnp.sum(weight, axis=1, keepdims=True) * full
    full_ref[...] = full.astype(BF)
    pack(full_ref, packer_ref, out_ref, cap)


def take_kernel(cap, pos_ref, in_ref, packer_ref, full_ref, own_ref, up_ref, down_ref):
    unpack(in_ref, packer_ref, full_ref, cap)
    wide = in_ref.shape[1]
    rows = full_ref.shape[0]
    half = rows // 2

    def quarter(j):
        return pl.ds(pl.multiple_of(lax.rem(pos_ref[0] + j, PARTS) * wide, wide), wide)

    own_ref[...] = full_ref[:, quarter(0)]
    up_ref[:rows, :] = full_ref[:, quarter(1)]
    up_ref[rows:, :] = full_ref[:half, quarter(2)]
    down_ref[:rows, :] = full_ref[:, quarter(3)]
    down_ref[rows:, :] = full_ref[half:, quarter(2)]


def forward_kernel(x_ref, wg_ref, wu_ref, pg_ref, pu_ref, h_ref):
    pre_gate = dot(x_ref[...], wg_ref[...])
    pre_up = dot(x_ref[...], wu_ref[...])
    pg_ref[...] = pre_gate
    pu_ref[...] = pre_up
    h_ref[...] = (pre_gate * jax.nn.sigmoid(pre_gate) * pre_up).astype(BF)


def backward_kernel(s_ref, wd_ref, pg_ref, pu_ref, g_ref, score_ref):
    n = pl.program_id(0)
    grad_hidden = dot_t(s_ref[...], wd_ref[...])
    pre_gate, pre_up = pg_ref[...], pu_ref[...]
    sig = jax.nn.sigmoid(pre_gate)
    act = pre_gate * sig
    hidden = (act * pre_up).astype(BF).astype(F32)
    g_ref[0] = (grad_hidden * pre_up * sig * (1.0 + pre_gate * (1.0 - sig))).astype(BF)
    g_ref[1] = (grad_hidden * act).astype(BF)
    part = jnp.sum(hidden * grad_hidden, axis=1, keepdims=True)

    @pl.when(n == 0)
    def _():
        score_ref[...] = part

    @pl.when(n > 0)
    def _():
        score_ref[...] += part


def back_kernel(cap, g_ref, wg_ref, wu_ref, score_ref, liner_ref, out_ref, full_ref):
    q = pl.program_id(0)
    wide = wg_ref.shape[0]
    cols = pl.ds(pl.multiple_of(q * wide, wide), wide)
    full_ref[:, cols] = (dot_t(g_ref[0], wg_ref[...]) + dot_t(g_ref[1], wu_ref[...])).astype(BF)

    @pl.when(q == pl.num_programs(0) - 1)
    def _():
        pack_lines(full_ref, liner_ref, out_ref, cap)
        slots = full_ref.shape[0]
        slot = lax.broadcasted_iota(jnp.int32, (slots, 128), 0).astype(F32)
        lane = lax.broadcasted_iota(jnp.int32, (slots, 128), 1).astype(F32)
        place = slot - cap * jnp.floor((slot + 0.5) * (1.0 / cap))
        spread = jnp.where(place == lane, score_ref[...], 0.0)
        owners = slots // cap
        first = lax.broadcasted_iota(jnp.int32, (owners, slots), 0) * cap
        col = lax.broadcasted_iota(jnp.int32, (owners, slots), 1)
        mine = jnp.where((col >= first) & (col < first + cap), 1.0, 0.0)
        found = jnp.dot(mine, spread, preferred_element_type=F32, precision=lax.Precision.HIGHEST).astype(BF)
        line = lax.broadcasted_iota(jnp.int32, (owners * LINES, owners), 0)
        owner = lax.broadcasted_iota(jnp.int32, (owners * LINES, owners), 1) * LINES
        out_ref[:, PARTS * cap // LINES * wide :] = dot(jnp.where(line == owner, 1.0, 0.0).astype(BF), found).astype(BF)


def finish_kernel(owners, cap, ids_ref, gates_ref, in_ref, liner_ref, gt_ref, gg_ref, full_ref):
    _, places, slots = route(ids_ref, owners, cap)
    unpack_lines(in_ref, liner_ref, full_ref, cap)
    pick = jnp.where(functools.reduce(jnp.logical_or, hits(slots, owners * cap)), 1.0, 0.0).astype(BF)
    gt_ref[...] = t_dot(pick, full_ref[...]).astype(BF)
    score = in_ref[:, in_ref.shape[1] - 128 :]
    lanes = lax.broadcasted_iota(jnp.int32, (128, ids_ref.shape[1]), 0)
    lines = lax.broadcasted_iota(jnp.int32, (owners * LINES, ids_ref.shape[1]), 0)
    for k, place in enumerate(places):
        chosen = jnp.where(lines == ids_ref[k : k + 1, :] * LINES, 1.0, 0.0).astype(BF)
        value = jnp.sum(jnp.where(lanes == place, t_dot(score, chosen), 0.0), axis=0, keepdims=True)
        gg_ref[k : k + 1, :] = (value / gates_ref[k : k + 1, :].astype(F32)).astype(BF)


def near_kernel(*refs):
    ins, outs = refs[:-3], refs[-3:]
    rows = ins[2].shape[0]
    gate = up = down = 0.0
    for i in range(0, len(ins), 4):
        x, s, h, g = ins[i : i + 4]
        gate = gate + t_dot(x[:rows, :], g[0])
        up = up + t_dot(x[:rows, :], g[1])
        down = down + t_dot(h[...], s[:rows, :])
    for out, total in zip(outs, (gate, up, down)):
        out[...] = total


def far_kernel(xa, xb, sa, sb, ha, hb, g0, g1, pgate, pup, pdown, gate, up, down):
    half = xa.shape[0]
    gate[...] = (pgate[...] + t_dot(xa[...], g0[:half, :]) + t_dot(xb[...], g0[half:, :])).astype(BF)
    up[...] = (pup[...] + t_dot(xa[...], g1[:half, :]) + t_dot(xb[...], g1[half:, :])).astype(BF)
    down[...] = (pdown[...] + t_dot(ha[...], sa[...]) + t_dot(hb[...], sb[...])).astype(BF)


def body(tokens, expert_ids, gates, cotangent, w_gate, w_up, w_down):
    toks, width = tokens.shape
    top = expert_ids.shape[1]
    owners = lax.axis_size("expert")
    groups = lax.axis_size("dp")
    cap = min(toks, 3 * toks * top // (2 * owners))
    slots = owners * cap
    half = slots // 2
    wg, wu, wd = w_gate[0], w_up[0], w_down[0]
    ff = wg.shape[1]
    wide = width // PARTS
    back_wide = PARTS * cap // LINES * wide + 128
    ids_t, gates_t = expert_ids.T, gates.T
    packer = jnp.asarray(permutation(cap), BF)
    liner = jnp.asarray(line_permutation(cap), BF)
    pos = lax.axis_index("dp").astype(jnp.int32).reshape(1)

    def go_up(v):
        return lax.ppermute(v, "dp", [(i, (i + 1) % groups) for i in range(groups)])

    def go_down(v):
        return lax.ppermute(v, "dp", [(i, (i - 1) % groups) for i in range(groups)])

    def exchange(v):
        v = v.reshape(owners, -1, v.shape[-1])
        v = lax.all_to_all(v, "expert", split_axis=0, concat_axis=0, tiled=True)
        return v.reshape(-1, v.shape[-1])

    def send(x, scaled):
        return call(
            functools.partial(send_kernel, owners, cap, scaled),
            [shape((slots * PARTS, wide))],
            [ids_t, gates_t, x, packer],
            scratch=[pltpu.VMEM((slots, width), BF)],
            flops=2 * slots * toks * width,
        )[0]

    def take(payload):
        return call(
            functools.partial(take_kernel, cap),
            [shape((slots, width)), shape((slots, wide)), shape((slots + half, wide)), shape((slots + half, wide))],
            [pos, payload, packer],
            specs=[SM, whole(payload.shape), whole(packer.shape)],
            flops=2 * slots * width * packer.shape[0],
        )

    by_col = lambda r: pl.BlockSpec((r, cut), lambda n: (0, n))
    cut = ff // 3

    sent_rows = exchange(send(tokens, False))
    sent_scaled = exchange(send(cotangent, True))

    rows, x_own, x_up, x_down = take(sent_rows)
    x_left, x_right = go_up(x_up), go_down(x_down)
    pre_gate, pre_up, hidden = call(
        forward_kernel,
        [shape((slots, ff), F32), shape((slots, ff), F32), shape((slots, ff))],
        [rows, wg, wu],
        specs=[whole((slots, width)), by_col(width), by_col(width)],
        out_specs=[by_col(slots), by_col(slots), by_col(slots)],
        grid=(3,),
        flops=4 * slots * width * ff,
    )
    hidden, x_left, x_right = lax.optimization_barrier((hidden, x_left, x_right))
    h_left, h_right = go_up(hidden), go_down(hidden)
    x_far = go_up(x_left[slots:]), go_down(x_right[slots:])
    h_left, h_right, x_far = lax.optimization_barrier((h_left, h_right, x_far))
    h_far = go_up(h_left[:half]), go_down(h_right[half:])
    sent_scaled, pre_gate, pre_up, h_far = lax.optimization_barrier((sent_scaled, pre_gate, pre_up, h_far))

    scaled, s_own, s_up, s_down = take(sent_scaled)
    s_left, s_right = go_up(s_up), go_down(s_down)
    grads, score = call(
        backward_kernel,
        [shape((2, slots, ff)), shape((slots, 1), F32)],
        [scaled, wd, pre_gate, pre_up],
        specs=[whole((slots, width)), pl.BlockSpec((cut, width), lambda n: (n, 0)), by_col(slots), by_col(slots)],
        out_specs=[pl.BlockSpec((2, slots, cut), lambda n: (0, 0, n)), whole((slots, 1))],
        grid=(3,),
        flops=2 * slots * width * ff,
    )
    g_left, g_right = go_up(grads), go_down(grads)
    by_row = pl.BlockSpec((wide, ff), lambda q: (q, 0))
    back = call(
        functools.partial(back_kernel, cap),
        [shape((owners * LINES, back_wide))],
        [grads, wg, wu, score, liner],
        specs=[whole(grads.shape), by_row, by_row, whole(score.shape), whole(liner.shape)],
        grid=(PARTS,),
        scratch=[pltpu.VMEM((slots, width), BF)],
        flops=4 * slots * width * ff,
    )[0]
    back_rows = exchange(back)
    s_far = go_up(s_left[slots:]), go_down(s_right[slots:])
    g_far = go_up(g_left[0]), go_down(g_right[1])
    grad_tokens, grad_gates_t = call(
        functools.partial(finish_kernel, owners, cap),
        [shape((toks, width)), shape((top, toks))],
        [ids_t, gates_t, back_rows, liner],
        scratch=[pltpu.VMEM((slots, width), BF)],
        flops=2 * slots * toks * width,
    )

    partial = call(
        near_kernel,
        [shape((wide, ff), F32), shape((wide, ff), F32), shape((ff, wide), F32)],
        [x_own, s_own, hidden, grads, x_left, s_left, h_left, g_left, x_right, s_right, h_right, g_right],
        flops=HINT * 6 * 3 * slots * wide * ff,
        limit=MOST,
    )
    grad_gate, grad_up, grad_down = call(
        far_kernel,
        [shape((wide, ff)), shape((wide, ff)), shape((ff, wide))],
        [*x_far, *s_far, *h_far, *g_far, *partial],
        flops=HINT * 6 * slots * wide * ff,
        limit=MOST,
    )
    return grad_tokens, grad_gates_t.T, grad_gate[None], grad_up[None], grad_down[None]


def solution(mesh):
    both = P(("dp", "expert"), None)
    held = P("expert", None, None)
    return jax.shard_map(
        body,
        mesh=mesh,
        in_specs=(both, both, both, both, held, held, held),
        out_specs=(both, both, P("expert", "dp", None), P("expert", "dp", None), P("expert", None, "dp")),
        check_vma=False,
    )
```

profile of v0, /device:TPU:6, one launch (start us, length us, event | category | flops | bytes accessed | tf_op | source)
XLA Modules:
  0.0 187.4 jit_solution(12215634719777307254)
XLA Ops:
  3.9 2.3 %shard_map.129 = bf16[1536,512]{1,0:T(8,128)(2,1)} custom-call(s32[2,128]{1,0:T(2,128)S(1)} %bitcast.28, bf16[2,128]{1,0:T(2,128)(2,1)S(1)} %bitcast.31, bf16[128,2048]{1,0:T(8,128)(2,1)S(1)} %copy-done.11, bf16[192,192]{1,0:T(8,128)(2,1)S(1)} %copy-done.5), custom_call_target="tpu_custom_call" | custom-call | flops 201326592 | bytes 2172416 | tf_op jit(solution)/shard_map/pallas_call | solution.py:40
  6.2 12.3 %all-to-all-start.1 = ((bf16[64,24,512]{2,1,0:T(8,128)(2,1)}), bf16[64,24,512]{2,1,0:T(8,128)(2,1)S(1)}, u32[]{:S(2)}, u32[]{:S(2)}) async-start(bf16[64,24,512]{2,1,0:T(8,128)(2,1)} %bitcast.5), calls=%async_computation.1 | async-start | bytes 3145728 | tf_op jit(solution)/shard_map/all_to_all | solution.py:282
  18.5 2.4 %shard_map.128 = bf16[1536,512]{1,0:T(8,128)(2,1)} custom-call(s32[2,128]{1,0:T(2,128)S(1)} %bitcast.29, bf16[2,128]{1,0:T(2,128)(2,1)S(1)} %bitcast.32, bf16[128,2048]{1,0:T(8,128)(2,1)S(1)} %copy-done.12, bf16[192,192]{1,0:T(8,128)(2,1)S(1)} %copy-done.6), custom_call_target="tpu_custom_call" | custom-call | flops 201326592 | bytes 2172416 | tf_op jit(solution)/shard_map/pallas_call | solution.py:40
  20.9 37.7 %all-to-all-done.1 = bf16[64,24,512]{2,1,0:T(8,128)(2,1)S(1)} async-done(((bf16[64,24,512]{2,1,0:T(8,128)(2,1)}), bf16[64,24,512]{2,1,0:T(8,128)(2,1)S(1)}, u32[]{:S(2)}, u32[]{:S(2)}) %all-to-all-start.1) | async-done | bytes 1572896 | tf_op jit(solution)/shard_map/all_to_all | solution.py:282
  58.6 5.3 %all-to-all-start = ((bf16[64,24,512]{2,1,0:T(8,128)(2,1)}), bf16[64,24,512]{2,1,0:T(8,128)(2,1)S(1)}, u32[]{:S(2)}, u32[]{:S(2)}) async-start(bf16[64,24,512]{2,1,0:T(8,128)(2,1)} %bitcast.3), calls=%async_computation | async-start | bytes 3145728 | tf_op jit(solution)/shard_map/all_to_all | solution.py:282
  65.2 1.5 collective-permute-start.1
  66.7 1.9 %copy-done.1 = bf16[1,2048,768]{2,1,0:T(8,128)(2,1)S(1)} copy-done((bf16[1,2048,768]{2,1,0:T(8,128)(2,1)S(1)}, bf16[1,2048,768]{2,1,0:T(8,128)(2,1)}, u32[]{:S(2)}) %copy-start.1) | copy-done | bytes 3145752
  68.6 1.9 %copy-done.3 = bf16[1,2048,768]{2,1,0:T(8,128)(2,1)S(1)} copy-done((bf16[1,2048,768]{2,1,0:T(8,128)(2,1)S(1)}, bf16[1,2048,768]{2,1,0:T(8,128)(2,1)}, u32[]{:S(2)}) %copy-start.3) | copy-done | bytes 3145752
  70.5 3.6 %shard_map.131 = (f32[384,768]{1,0:T(8,128)S(1)}, f32[384,768]{1,0:T(8,128)S(1)}, bf16[384,768]{1,0:T(8,128)(2,1)S(1)}) custom-call(bf16[384,2048]{1,0:T(8,128)(2,1)S(1)} %get-tuple-element.38.x_ref, bf16[2048,768]{1,0:T(8,128)(2,1)S(1)} %bitcast.24, bf16[2048,768]{1,0:T(8,128)(2,1)S(1)} %bitcast.26), custom_call_target="tpu_custom_call" | custom-call | flops 2415919104 | bytes 10813440 | tf_op jit(solution)/shard_map/pallas_call | solution.py:40
  75.2 4.8 %collective-permute-done.refs_4_ = bf16[576,512]{1,0:T(8,128)(2,1)S(1)} collective-permute-done((bf16[576,512]{1,0:T(8,128)(2,1)S(1)}, bf16[576,512]{1,0:T(8,128)(2,1)S(1)}, u32[]{:S(2)}, u32[]{:S(2)}) %collective-permute-start) | collective-permute-done | bytes 589856 | tf_op jit(solution)/shard_map/ppermute | solution.py:275
  81.8 1.7 collective-permute-start.3
  83.5 1.6 collective-permute-start.4
  85.7 14.1 %collective-permute-done.4.xa = bf16[192,512]{1,0:T(8,128)(2,1)S(1)} collective-permute-done((bf16[192,512]{1,0:T(8,128)(2,1)S(1)}, bf16[192,512]{1,0:T(8,128)(2,1)S(1)}, u32[]{:S(2)}, u32[]{:S(2)}) %collective-permute-start.4) | collective-permute-done | bytes 196640 | tf_op jit(solution)/shard_map/ppermute | solution.py:275
  99.7 1.6 collective-permute-done.5.xb
  102.2 1.6 collective-permute-start.7
  104.1 4.3 %collective-permute-done.6.ha = bf16[192,768]{1,0:T(8,128)(2,1)S(1)} collective-permute-done((bf16[192,768]{1,0:T(8,128)(2,1)S(1)}, bf16[192,768]{1,0:T(8,128)(2,1)S(1)}, u32[]{:S(2)}, u32[]{:S(2)}) %collective-permute-start.6) | collective-permute-done | bytes 294944 | tf_op jit(solution)/shard_map/ppermute | solution.py:275
  108.4 2.1 %collective-permute-done.7.hb = bf16[192,768]{1,0:T(8,128)(2,1)S(1)} collective-permute-done((bf16[192,768]{1,0:T(8,128)(2,1)S(1)}, bf16[192,768]{1,0:T(8,128)(2,1)S(1)}, u32[]{:S(2)}, u32[]{:S(2)}) %collective-permute-start.7) | collective-permute-done | bytes 294944 | tf_op jit(solution)/shard_map/ppermute | solution.py:278
  111.2 1.7 shard_map.132
  113.6 1.9 %copy-done = bf16[1,768,2048]{2,1,0:T(8,128)(2,1)S(1)} copy-done((bf16[1,768,2048]{2,1,0:T(8,128)(2,1)S(1)}, bf16[1,768,2048]{2,1,0:T(8,128)(2,1)}, u32[]{:S(2)}) %copy-start) | copy-done | bytes 3145752
  116.8 3.3 %shard_map.133 = (bf16[2,384,768]{2,1,0:T(8,128)(2,1)}, f32[384,1]{1,0:T(8,128)S(1)}) custom-call(bf16[384,2048]{1,0:T(8,128)(2,1)S(1)} %get-tuple-element.50.s_ref, bf16[768,2048]{1,0:T(8,128)(2,1)S(1)} %bitcast.23, f32[384,768]{1,0:T(8,128)S(1)} %copy-done.8, f32[384,768]{1,0:T(8,128)S(1)} %copy-done.10), custom_call_target="tpu_custom_call" | custom-call | flops 1207959552 | bytes 8259072 | tf_op jit(solution)/shard_map/pallas_call | solution.py:40
  120.1 2.0 %collective-permute-start.14 = (bf16[2,384,768]{2,1,0:T(8,128)(2,1)}, bf16[2,384,768]{2,1,0:T(8,128)(2,1)}, u32[]{:S(2)}, u32[]{:S(2)}) collective-permute-start(bf16[2,384,768]{2,1,0:T(8,128)(2,1)} %get-tuple-element.53.g_ref.refs_3_), channel_id=1, source_target_pairs={{0,192},{64,0},{128,64},{192,128},{1,193},{65,1},{129,65},{193,129... | collective-permute-start | bytes 3538952 | tf_op jit(solution)/shard_map/ppermute | solution.py:278
  122.2 3.1 %collective-permute-start.8 = (bf16[576,512]{1,0:T(8,128)(2,1)}, bf16[576,512]{1,0:T(8,128)(2,1)S(1)}, u32[]{:S(2)}, u32[]{:S(2)}) collective-permute-start(bf16[576,512]{1,0:T(8,128)(2,1)} %get-tuple-element.59), channel_id=1, source_target_pairs={{0,64},{64,128},{128,192},{192,0},{1,65},{65,129},{129,193},{193,1... | collective-permute-start | bytes 1769480 | tf_op jit(solution)/shard_map/ppermute | solution.py:275
  125.4 6.7 %shard_map.134 = bf16[512,1664]{1,0:T(8,128)(2,1)} custom-call(bf16[2,384,768]{2,1,0:T(8,128)(2,1)} %get-tuple-element.53.g_ref.refs_3_, bf16[2048,768]{1,0:T(8,128)(2,1)S(1)} %bitcast.25, bf16[2048,768]{1,0:T(8,128)(2,1)S(1)} %bitcast.27, f32[384,1]{1,0:T(8,128)S(1)} %get-tuple-element.54.score_ref, bf16[192,192]{1,0:T(8,128)(2,1)S(1)} %copy-done.13), custom_call_target="tpu_custom_call" | custom-call | flops 2415919104 | bytes 9250304 | tf_op jit(solution)/shard_map/pallas_call | solution.py:40
  132.0 10.6 %all-to-all-start.2 = ((bf16[64,8,1664]{2,1,0:T(8,128)(2,1)}), bf16[64,8,1664]{2,1,0:T(8,128)(2,1)S(1)}, u32[]{:S(2)}, u32[]{:S(2)}) async-start(bf16[64,8,1664]{2,1,0:T(8,128)(2,1)} %bitcast.10), calls=%async_computation.2 | async-start | bytes 3407872 | tf_op jit(solution)/shard_map/all_to_all | solution.py:282
  142.7 16.5 %collective-permute-done.10.refs_9_ = bf16[576,512]{1,0:T(8,128)(2,1)S(1)} collective-permute-done((bf16[576,512]{1,0:T(8,128)(2,1)}, bf16[576,512]{1,0:T(8,128)(2,1)S(1)}, u32[]{:S(2)}, u32[]{:S(2)}) %collective-permute-start.10) | collective-permute-done | bytes 589856 | tf_op jit(solution)/shard_map/ppermute | solution.py:278
  159.1 1.9 %collective-permute-start.11 = (bf16[192,512]{1,0:T(8,128)(2,1)S(1)}, bf16[192,512]{1,0:T(8,128)(2,1)S(1)}, u32[]{:S(2)}, u32[]{:S(2)}) collective-permute-start(bf16[192,512]{1,0:T(8,128)(2,1)S(1)} %slice.33), channel_id=1, source_target_pairs={{0,192},{64,0},{128,64},{192,128},{1,193},{65,1},{129,65},{193,129... | collective-permute-start | bytes 589832 | tf_op jit(solution)/shard_map/ppermute | solution.py:278
  161.1 1.5 collective-permute-start.9
  165.0 2.2 %collective-permute-start.15 = (bf16[384,768]{1,0:T(8,128)(2,1)S(1)}, bf16[384,768]{1,0:T(8,128)(2,1)}, u32[]{:S(2)}, u32[]{:S(2)}) collective-permute-start(bf16[384,768]{1,0:T(8,128)(2,1)S(1)} %slice_bitcast_fusion), channel_id=1, source_target_pairs={{0,192},{64,0},{128,64},{192,128},{1,193},{65,1},{129,65},{193,129... | collective-permute-start | bytes 1769480 | tf_op jit(solution)/shard_map/ppermute | solution.py:278
  167.2 8.8 %shard_map.136 = (f32[512,768]{1,0:T(8,128)}, f32[512,768]{1,0:T(8,128)}, f32[768,512]{1,0:T(8,128)}) custom-call(bf16[384,512]{1,0:T(8,128)(2,1)} %copy-done.19, bf16[384,512]{1,0:T(8,128)(2,1)} %copy-done.20, bf16[384,768]{1,0:T(8,128)(2,1)} %copy-done.18, bf16[2,384,768]{2,1,0:T(8,128)(2,1)} %get-tuple-element.53.g_ref.refs_3_, ...), custom_call_target="tpu_custom_call" | custom-call | flops 27179089920 | bytes 13172736 | tf_op jit(solution)/shard_map/pallas_call | solution.py:40
  176.8 2.0 %collective-permute-done.15.g1 = bf16[384,768]{1,0:T(8,128)(2,1)} collective-permute-done((bf16[384,768]{1,0:T(8,128)(2,1)S(1)}, bf16[384,768]{1,0:T(8,128)(2,1)}, u32[]{:S(2)}, u32[]{:S(2)}) %collective-permute-start.15) | collective-permute-done | bytes 589856 | tf_op jit(solution)/shard_map/ppermute | solution.py:278
  178.8 5.5 %shard_map.137 = (bf16[512,768]{1,0:T(8,128)(2,1)}, bf16[512,768]{1,0:T(8,128)(2,1)}, bf16[768,512]{1,0:T(8,128)(2,1)}) custom-call(bf16[192,512]{1,0:T(8,128)(2,1)} %copy-done.29, bf16[192,512]{1,0:T(8,128)(2,1)} %copy-done.30, bf16[192,512]{1,0:T(8,128)(2,1)} %copy-done.32, bf16[192,512]{1,0:T(8,128)(2,1)} %copy-done.31, bf16[192,768]{1,0:T(8,128)(2,1)} %copy-done.27, ...), custom_call_target="tpu_custom_call" | custom-call | flops 9059696640 | bytes 9633792 | tf_op jit(solution)/shard_map/pallas_call | solution.py:40
  185.6 1.8 shard_map.135
  (90 shorter events, 16.2 us)
Async XLA Ops:
  6.2 12.3 %copy-start.6 = (bf16[192,192]{1,0:T(8,128)(2,1)S(1)}, bf16[192,192]{1,0:T(8,128)(2,1)}, u32[]{:S(2)}) copy-start(bf16[192,192]{1,0:T(8,128)(2,1)} %constant.10.clone.packer_ref) | copy-start | bytes 221188
  6.2 12.3 %copy-start.12 = (bf16[128,2048]{1,0:T(8,128)(2,1)S(1)}, bf16[128,2048]{1,0:T(8,128)(2,1)}, u32[]{:S(2)}) copy-start(bf16[128,2048]{1,0:T(8,128)(2,1)} %x_ref.2) | copy-start | bytes 1572868
  6.2 12.3 %copy-start.15 = (s32[128,2]{0,1:T(2,128)S(1)}, s32[128,2]{0,1:T(2,128)}, u32[]{:S(2)}) copy-start(s32[128,2]{0,1:T(2,128)} %param.10) | copy-start | bytes 3076
  6.2 12.3 %copy-start.17 = (bf16[128,2]{0,1:T(2,128)(2,1)S(1)}, bf16[128,2]{0,1:T(2,128)(2,1)}, u32[]{:S(2)}) copy-start(bf16[128,2]{0,1:T(2,128)(2,1)} %param.11) | copy-start | bytes 1540
  6.2 52.4 %all-to-all-start.1 = ((bf16[64,24,512]{2,1,0:T(8,128)(2,1)}), bf16[64,24,512]{2,1,0:T(8,128)(2,1)S(1)}, u32[]{:S(2)}, u32[]{:S(2)}) async-start(bf16[64,24,512]{2,1,0:T(8,128)(2,1)} %bitcast.5), calls=%async_computation.1 | async-start | bytes 3145728 | tf_op jit(solution)/shard_map/all_to_all | solution.py:282
  58.6 45.5 %all-to-all-start = ((bf16[64,24,512]{2,1,0:T(8,128)(2,1)}), bf16[64,24,512]{2,1,0:T(8,128)(2,1)S(1)}, u32[]{:S(2)}, u32[]{:S(2)}) async-start(bf16[64,24,512]{2,1,0:T(8,128)(2,1)} %bitcast.3), calls=%async_computation | async-start | bytes 3145728 | tf_op jit(solution)/shard_map/all_to_all | solution.py:282
  64.6 9.5 %copy-start.19 = (bf16[384,512]{1,0:T(8,128)(2,1)}, bf16[384,512]{1,0:T(8,128)(2,1)S(1)}, u32[]{:S(2)}) copy-start(bf16[384,512]{1,0:T(8,128)(2,1)S(1)} %get-tuple-element.63.refs_0_) | copy-start | bytes 1179652
  64.6 15.4 %collective-permute-start = (bf16[576,512]{1,0:T(8,128)(2,1)S(1)}, bf16[576,512]{1,0:T(8,128)(2,1)S(1)}, u32[]{:S(2)}, u32[]{:S(2)}) collective-permute-start(bf16[576,512]{1,0:T(8,128)(2,1)S(1)} %get-tuple-element.42), channel_id=1, source_target_pairs={{0,64},{64,128},{128,192},{192,0},{1,65},{65,129},{129,193},{193,1... | collective-permute-start | bytes 1769480 | tf_op jit(solution)/shard_map/ppermute | solution.py:275
  65.2 16.2 %collective-permute-start.1 = (bf16[576,512]{1,0:T(8,128)(2,1)S(1)}, bf16[576,512]{1,0:T(8,128)(2,1)S(1)}, u32[]{:S(2)}, u32[]{:S(2)}) collective-permute-start(bf16[576,512]{1,0:T(8,128)(2,1)S(1)} %get-tuple-element.43), channel_id=1, source_target_pairs={{0,192},{64,0},{128,64},{192,128},{1,193},{65,1},{129,65},{193,129... | collective-permute-start | bytes 1769480 | tf_op jit(solution)/shard_map/ppermute | solution.py:278
  75.2 26.9 %copy-start.7 = (f32[384,768]{1,0:T(8,128)}, f32[384,768]{1,0:T(8,128)S(1)}, u32[]{:S(2)}) copy-start(f32[384,768]{1,0:T(8,128)S(1)} %get-tuple-element.51.pg_ref) | copy-start | bytes 3538948
  75.2 26.9 %copy-start.18 = (bf16[384,768]{1,0:T(8,128)(2,1)}, bf16[384,768]{1,0:T(8,128)(2,1)S(1)}, u32[]{:S(2)}) copy-start(bf16[384,768]{1,0:T(8,128)(2,1)S(1)} %get-tuple-element.44.refs_2_) | copy-start | bytes 1769476
  80.0 21.4 %copy-start.23 = (bf16[576,512]{1,0:T(8,128)(2,1)}, bf16[576,512]{1,0:T(8,128)(2,1)S(1)}, u32[]{:S(2)}) copy-start(bf16[576,512]{1,0:T(8,128)(2,1)S(1)} %collective-permute-done.refs_4_) | copy-start | bytes 1769476
  81.4 20.7 %copy-start.24 = (bf16[576,512]{1,0:T(8,128)(2,1)}, bf16[576,512]{1,0:T(8,128)(2,1)S(1)}, u32[]{:S(2)}) copy-start(bf16[576,512]{1,0:T(8,128)(2,1)S(1)} %collective-permute-done.1.refs_8_) | copy-start | bytes 1769476
  81.4 19.9 %collective-permute-start.2 = (bf16[384,768]{1,0:T(8,128)(2,1)S(1)}, bf16[384,768]{1,0:T(8,128)(2,1)S(1)}, u32[]{:S(2)}, u32[]{:S(2)}) collective-permute-start(bf16[384,768]{1,0:T(8,128)(2,1)S(1)} %get-tuple-element.44.refs_2_), channel_id=1, source_target_pairs={{0,64},{64,128},{128,192},{192,0},{1,65},{65,129},{129,193},{193,1... | collective-permute-start | bytes 1769480 | tf_op jit(solution)/shard_map/ppermute | solution.py:275
  81.8 19.6 %collective-permute-start.3 = (bf16[384,768]{1,0:T(8,128)(2,1)S(1)}, bf16[384,768]{1,0:T(8,128)(2,1)S(1)}, u32[]{:S(2)}, u32[]{:S(2)}) collective-permute-start(bf16[384,768]{1,0:T(8,128)(2,1)S(1)} %get-tuple-element.44.refs_2_), channel_id=1, source_target_pairs={{0,192},{64,0},{128,64},{192,128},{1,193},{65,1},{129,65},{193,129... | collective-permute-start | bytes 1769480 | tf_op jit(solution)/shard_map/ppermute | solution.py:278
  83.5 16.3 %collective-permute-start.4 = (bf16[192,512]{1,0:T(8,128)(2,1)S(1)}, bf16[192,512]{1,0:T(8,128)(2,1)S(1)}, u32[]{:S(2)}, u32[]{:S(2)}) collective-permute-start(bf16[192,512]{1,0:T(8,128)(2,1)S(1)} %slice.24), channel_id=1, source_target_pairs={{0,64},{64,128},{128,192},{192,0},{1,65},{65,129},{129,193},{193,1... | collective-permute-start | bytes 589832 | tf_op jit(solution)/shard_map/ppermute | solution.py:275
  85.1 16.2 %collective-permute-start.5 = (bf16[192,512]{1,0:T(8,128)(2,1)S(1)}, bf16[192,512]{1,0:T(8,128)(2,1)S(1)}, u32[]{:S(2)}, u32[]{:S(2)}) collective-permute-start(bf16[192,512]{1,0:T(8,128)(2,1)S(1)} %slice.25), channel_id=1, source_target_pairs={{0,192},{64,0},{128,64},{192,128},{1,193},{65,1},{129,65},{193,129... | collective-permute-start | bytes 589832 | tf_op jit(solution)/shard_map/ppermute | solution.py:278
  101.4 9.1 %copy-start.22 = (bf16[384,768]{1,0:T(8,128)(2,1)}, bf16[384,768]{1,0:T(8,128)(2,1)S(1)}, u32[]{:S(2)}) copy-start(bf16[384,768]{1,0:T(8,128)(2,1)S(1)} %collective-permute-done.3.refs_10_) | copy-start | bytes 1769476
  101.4 7.0 %collective-permute-start.6 = (bf16[192,768]{1,0:T(8,128)(2,1)S(1)}, bf16[192,768]{1,0:T(8,128)(2,1)S(1)}, u32[]{:S(2)}, u32[]{:S(2)}) collective-permute-start(bf16[192,768]{1,0:T(8,128)(2,1)S(1)} %slice.26), channel_id=1, source_target_pairs={{0,64},{64,128},{128,192},{192,0},{1,65},{65,129},{129,193},{193,1... | collective-permute-start | bytes 884744 | tf_op jit(solution)/shard_map/ppermute | solution.py:275
  102.2 8.2 %collective-permute-start.7 = (bf16[192,768]{1,0:T(8,128)(2,1)S(1)}, bf16[192,768]{1,0:T(8,128)(2,1)S(1)}, u32[]{:S(2)}, u32[]{:S(2)}) collective-permute-start(bf16[192,768]{1,0:T(8,128)(2,1)S(1)} %slice.27), channel_id=1, source_target_pairs={{0,192},{64,0},{128,64},{192,128},{1,193},{65,1},{129,65},{193,129... | collective-permute-start | bytes 884744 | tf_op jit(solution)/shard_map/ppermute | solution.py:278
  104.1 9.5 %copy-start.8 = (f32[384,768]{1,0:T(8,128)S(1)}, f32[384,768]{1,0:T(8,128)}, u32[]{:S(2)}) copy-start(f32[384,768]{1,0:T(8,128)} %copy-done.7) | copy-start | bytes 3538948
  108.4 11.7 %copy-start.27 = (bf16[192,768]{1,0:T(8,128)(2,1)}, bf16[192,768]{1,0:T(8,128)(2,1)S(1)}, u32[]{:S(2)}) copy-start(bf16[192,768]{1,0:T(8,128)(2,1)S(1)} %collective-permute-done.6.ha) | copy-start | bytes 884740
  116.8 8.6 %copy-start.13 = (bf16[192,192]{1,0:T(8,128)(2,1)S(1)}, bf16[192,192]{1,0:T(8,128)(2,1)}, u32[]{:S(2)}) copy-start(bf16[192,192]{1,0:T(8,128)(2,1)} %constant.11.clone.liner_ref) | copy-start | bytes 221188
  120.1 42.5 %collective-permute-start.12 = (bf16[2,384,768]{2,1,0:T(8,128)(2,1)}, bf16[2,384,768]{2,1,0:T(8,128)(2,1)}, u32[]{:S(2)}, u32[]{:S(2)}) collective-permute-start(bf16[2,384,768]{2,1,0:T(8,128)(2,1)} %get-tuple-element.53.g_ref.refs_3_), channel_id=1, source_target_pairs={{0,64},{64,128},{128,192},{192,0},{1,65},{65,129},{129,193},{193,1... | collective-permute-start | bytes 3538952 | tf_op jit(solution)/shard_map/ppermute | solution.py:275
  120.1 43.8 %collective-permute-start.14 = (bf16[2,384,768]{2,1,0:T(8,128)(2,1)}, bf16[2,384,768]{2,1,0:T(8,128)(2,1)}, u32[]{:S(2)}, u32[]{:S(2)}) collective-permute-start(bf16[2,384,768]{2,1,0:T(8,128)(2,1)} %get-tuple-element.53.g_ref.refs_3_), channel_id=1, source_target_pairs={{0,192},{64,0},{128,64},{192,128},{1,193},{65,1},{129,65},{193,129... | collective-permute-start | bytes 3538952 | tf_op jit(solution)/shard_map/ppermute | solution.py:278
  122.1 37.0 %collective-permute-start.10 = (bf16[576,512]{1,0:T(8,128)(2,1)}, bf16[576,512]{1,0:T(8,128)(2,1)S(1)}, u32[]{:S(2)}, u32[]{:S(2)}) collective-permute-start(bf16[576,512]{1,0:T(8,128)(2,1)} %get-tuple-element.60), channel_id=1, source_target_pairs={{0,192},{64,0},{128,64},{192,128},{1,193},{65,1},{129,65},{193,129... | collective-permute-start | bytes 1769480 | tf_op jit(solution)/shard_map/ppermute | solution.py:278
  122.2 38.8 %collective-permute-start.8 = (bf16[576,512]{1,0:T(8,128)(2,1)}, bf16[576,512]{1,0:T(8,128)(2,1)S(1)}, u32[]{:S(2)}, u32[]{:S(2)}) collective-permute-start(bf16[576,512]{1,0:T(8,128)(2,1)} %get-tuple-element.59), channel_id=1, source_target_pairs={{0,64},{64,128},{128,192},{192,0},{1,65},{65,129},{129,193},{193,1... | collective-permute-start | bytes 1769480 | tf_op jit(solution)/shard_map/ppermute | solution.py:275
  132.0 53.5 %all-to-all-start.2 = ((bf16[64,8,1664]{2,1,0:T(8,128)(2,1)}), bf16[64,8,1664]{2,1,0:T(8,128)(2,1)S(1)}, u32[]{:S(2)}, u32[]{:S(2)}) async-start(bf16[64,8,1664]{2,1,0:T(8,128)(2,1)} %bitcast.10), calls=%async_computation.2 | async-start | bytes 3407872 | tf_op jit(solution)/shard_map/all_to_all | solution.py:282
  159.1 16.8 %collective-permute-start.11 = (bf16[192,512]{1,0:T(8,128)(2,1)S(1)}, bf16[192,512]{1,0:T(8,128)(2,1)S(1)}, u32[]{:S(2)}, u32[]{:S(2)}) collective-permute-start(bf16[192,512]{1,0:T(8,128)(2,1)S(1)} %slice.33), channel_id=1, source_target_pairs={{0,192},{64,0},{128,64},{192,128},{1,193},{65,1},{129,65},{193,129... | collective-permute-start | bytes 589832 | tf_op jit(solution)/shard_map/ppermute | solution.py:278
  161.1 14.9 %collective-permute-start.9 = (bf16[192,512]{1,0:T(8,128)(2,1)S(1)}, bf16[192,512]{1,0:T(8,128)(2,1)S(1)}, u32[]{:S(2)}, u32[]{:S(2)}) collective-permute-start(bf16[192,512]{1,0:T(8,128)(2,1)S(1)} %slice.32), channel_id=1, source_target_pairs={{0,64},{64,128},{128,192},{192,0},{1,65},{65,129},{129,193},{193,1... | collective-permute-start | bytes 589832 | tf_op jit(solution)/shard_map/ppermute | solution.py:275
  163.7 13.1 %collective-permute-start.13 = (bf16[384,768]{1,0:T(8,128)(2,1)S(1)}, bf16[384,768]{1,0:T(8,128)(2,1)}, u32[]{:S(2)}, u32[]{:S(2)}) collective-permute-start(bf16[384,768]{1,0:T(8,128)(2,1)S(1)} %slice_bitcast_fusion.1), channel_id=1, source_target_pairs={{0,64},{64,128},{128,192},{192,0},{1,65},{65,129},{129,193},{193,1... | collective-permute-start | bytes 1769480 | tf_op jit(solution)/shard_map/ppermute | solution.py:275
  165.0 13.9 %collective-permute-start.15 = (bf16[384,768]{1,0:T(8,128)(2,1)S(1)}, bf16[384,768]{1,0:T(8,128)(2,1)}, u32[]{:S(2)}, u32[]{:S(2)}) collective-permute-start(bf16[384,768]{1,0:T(8,128)(2,1)S(1)} %slice_bitcast_fusion), channel_id=1, source_target_pairs={{0,192},{64,0},{128,64},{192,128},{1,193},{65,1},{129,65},{193,129... | collective-permute-start | bytes 1769480 | tf_op jit(solution)/shard_map/ppermute | solution.py:278
  (20 other events, 45.7 us)
where the time goes:
time: 188 us; the launch traced here: 187 us
  waiting for transfers between devices  86.8 us (46%)
  starting transfers between devices  47.5 us (25%)
  Pallas kernels  36.7 us (20%)
  local copies, waits for them, and re-layouts  15.5 us (8%)
    all_to_all x3, waiting for transfers between devices, exchange(): v = lax.all_to_all(v, 'expert', split_axis=0, concat_axis=0, tiled=True)  39.1 us
    pallas_call x10, Pallas kernels, call(): pl.pallas_call(kernel, out_shape=outs, grid=grid, in_specs=specs or [whol...  36.7 us
    all_to_all x3, starting transfers between devices, exchange(): v = lax.all_to_all(v, 'expert', split_axis=0, concat_axis=0, tiled=True)  28.2 us
    ppermute x8, waiting for transfers between devices, go_up(): return lax.ppermute(v, 'dp', [(i, (i + 1) % groups) for i in range(groups)])  24.1 us
    ppermute x8, waiting for transfers between devices, go_down(): return lax.ppermute(v, 'dp', [(i, (i - 1) % groups) for i in range(groups)])  23.6 us
    unnamed x66, local copies, waits for them, and re-layouts  13.2 us
    ppermute x8, starting transfers between devices, go_down(): return lax.ppermute(v, 'dp', [(i, (i - 1) % groups) for i in range(groups)])  11.6 us
    ppermute x8, starting transfers between devices, go_up(): return lax.ppermute(v, 'dp', [(i, (i + 1) % groups) for i in range(groups)])  7.72 us
  transfers between devices with their start and end apart: 19, of which 12 were waited for; matrix products, arithmetic and copies ran while one was open for 1% of the time, Pallas kernels for 15%

commit v1 on v0

--- a/solution.py
+++ b/solution.py
@@ -152,20 +152,12 @@
     pack(full_ref, packer_ref, out_ref, cap)
 
 
-def take_kernel(cap, pos_ref, in_ref, packer_ref, full_ref, own_ref, up_ref, down_ref):
+def take_kernel(cap, pos_ref, in_ref, packer_ref, full_ref, *piece_refs):
     unpack(in_ref, packer_ref, full_ref, cap)
     wide = in_ref.shape[1]
-    rows = full_ref.shape[0]
-    half = rows // 2
-
-    def quarter(j):
-        return pl.ds(pl.multiple_of(lax.rem(pos_ref[0] + j, PARTS) * wide, wide), wide)
-
-    own_ref[...] = full_ref[:, quarter(0)]
-    up_ref[:rows, :] = full_ref[:, quarter(1)]
-    up_ref[rows:, :] = full_ref[:half, quarter(2)]
-    down_ref[:rows, :] = full_ref[:, quarter(3)]
-    down_ref[rows:, :] = full_ref[half:, quarter(2)]
+    for j, piece in enumerate(piece_refs):
+        at = pl.multiple_of(lax.rem(pos_ref[0] + j, PARTS) * wide, wide)
+        piece[...] = full_ref[:, pl.ds(at, wide)]
 
 
 def forward_kernel(x_ref, wg_ref, wu_ref, pg_ref, pu_ref, h_ref):
@@ -176,9 +168,15 @@
     h_ref[...] = (pre_gate * jax.nn.sigmoid(pre_gate) * pre_up).astype(BF)
 
 
-def backward_kernel(s_ref, wd_ref, pg_ref, pu_ref, g_ref, score_ref):
+def backward_kernel(cap, pos_ref, in_ref, packer_ref, wd_ref, pg_ref, pu_ref, g_ref, score_ref, *rest):
+    *piece_refs, full_ref = rest
     n = pl.program_id(0)
-    grad_hidden = dot_t(s_ref[...], wd_ref[...])
+
+    @pl.when(n == 0)
+    def _():
+        take_kernel(cap, pos_ref, in_ref, packer_ref, full_ref, *piece_refs)
+
+    grad_hidden = dot_t(full_ref[...], wd_ref[...])
     pre_gate, pre_up = pg_ref[...], pu_ref[...]
     sig = jax.nn.sigmoid(pre_gate)
     act = pre_gate * sig
@@ -235,23 +233,18 @@
 
 
 def near_kernel(*refs):
-    ins, outs = refs[:-3], refs[-3:]
-    rows = ins[2].shape[0]
-    gate = up = down = 0.0
-    for i in range(0, len(ins), 4):
-        x, s, h, g = ins[i : i + 4]
-        gate = gate + t_dot(x[:rows, :], g[0])
-        up = up + t_dot(x[:rows, :], g[1])
-        down = down + t_dot(h[...], s[:rows, :])
-    for out, total in zip(outs, (gate, up, down)):
-        out[...] = total
-
-
-def far_kernel(xa, xb, sa, sb, ha, hb, g0, g1, pgate, pup, pdown, gate, up, down):
-    half = xa.shape[0]
-    gate[...] = (pgate[...] + t_dot(xa[...], g0[:half, :]) + t_dot(xb[...], g0[half:, :])).astype(BF)
-    up[...] = (pup[...] + t_dot(xa[...], g1[:half, :]) + t_dot(xb[...], g1[half:, :])).astype(BF)
-    down[...] = (pdown[...] + t_dot(ha[...], sa[...]) + t_dot(hb[...], sb[...])).astype(BF)
+    ins, outs = refs[:-2], refs[-2:]
+    for k, out in enumerate(outs):
+        out[...] = sum(t_dot(x[...], g[k]) for x, g in zip(ins[::2], ins[1::2]))
+
+
+def last_kernel(x, g0, g1, pgate, pup, *refs):
+    near, (ha, hb, s), (gate, up, down) = refs[:-6], refs[-6:-3], refs[-3:]
+    half = ha.shape[0]
+    gate[...] = (pgate[...] + t_dot(x[...], g0[...])).astype(BF)
+    up[...] = (pup[...] + t_dot(x[...], g1[...])).astype(BF)
+    far = t_dot(ha[...], s[:half, :]) + t_dot(hb[...], s[half:, :])
+    down[...] = (sum(t_dot(h[...], v[...]) for h, v in zip(near[::2], near[1::2])) + far).astype(BF)
 
 
 def body(tokens, expert_ids, gates, cotangent, w_gate, w_up, w_down):
@@ -274,6 +267,9 @@
     def go_up(v):
         return lax.ppermute(v, "dp", [(i, (i + 1) % groups) for i in range(groups)])
 
+    def go_across(v):
+        return lax.ppermute(v, "dp", [(i, (i + 2) % groups) for i in range(groups)])
+
     def go_down(v):
         return lax.ppermute(v, "dp", [(i, (i - 1) % groups) for i in range(groups)])
 
@@ -289,12 +285,13 @@
             [ids_t, gates_t, x, packer],
             scratch=[pltpu.VMEM((slots, width), BF)],
             flops=2 * slots * toks * width,
+            limit=MOST,
         )[0]
 
     def take(payload):
         return call(
             functools.partial(take_kernel, cap),
-            [shape((slots, width)), shape((slots, wide)), shape((slots + half, wide)), shape((slots + half, wide))],
+            [shape((slots, width))] + [shape((slots, wide))] * PARTS,
             [pos, payload, packer],
             specs=[SM, whole(payload.shape), whole(packer.shape)],
             flops=2 * slots * width * packer.shape[0],
@@ -306,8 +303,8 @@
     sent_rows = exchange(send(tokens, False))
     sent_scaled = exchange(send(cotangent, True))
 
-    rows, x_own, x_up, x_down = take(sent_rows)
-    x_left, x_right = go_up(x_up), go_down(x_down)
+    rows, x_own, x_next, x_across, x_last = take(sent_rows)
+    x_left, x_right, x_far = go_up(x_next), go_down(x_last), go_across(x_across)
     pre_gate, pre_up, hidden = call(
         forward_kernel,
         [shape((slots, ff), F32), shape((slots, ff), F32), shape((slots, ff))],
@@ -316,25 +313,25 @@
         out_specs=[by_col(slots), by_col(slots), by_col(slots)],
         grid=(3,),
         flops=4 * slots * width * ff,
+        limit=MOST,
     )
     hidden, x_left, x_right = lax.optimization_barrier((hidden, x_left, x_right))
     h_left, h_right = go_up(hidden), go_down(hidden)
-    x_far = go_up(x_left[slots:]), go_down(x_right[slots:])
-    h_left, h_right, x_far = lax.optimization_barrier((h_left, h_right, x_far))
+    sent_scaled, x_far, h_left, h_right = lax.optimization_barrier((sent_scaled, x_far, h_left, h_right))
     h_far = go_up(h_left[:half]), go_down(h_right[half:])
-    sent_scaled, pre_gate, pre_up, h_far = lax.optimization_barrier((sent_scaled, pre_gate, pre_up, h_far))
-
-    scaled, s_own, s_up, s_down = take(sent_scaled)
-    s_left, s_right = go_up(s_up), go_down(s_down)
-    grads, score = call(
-        backward_kernel,
-        [shape((2, slots, ff)), shape((slots, 1), F32)],
-        [scaled, wd, pre_gate, pre_up],
-        specs=[whole((slots, width)), pl.BlockSpec((cut, width), lambda n: (n, 0)), by_col(slots), by_col(slots)],
-        out_specs=[pl.BlockSpec((2, slots, cut), lambda n: (0, 0, n)), whole((slots, 1))],
+
+    grads, score, s_own, s_next, s_across, s_last = call(
+        functools.partial(backward_kernel, cap),
+        [shape((2, slots, ff)), shape((slots, 1), F32)] + [shape((slots, wide))] * PARTS,
+        [pos, sent_scaled, packer, wd, pre_gate, pre_up],
+        specs=[SM, whole(sent_scaled.shape), whole(packer.shape), pl.BlockSpec((cut, width), lambda n: (n, 0)), by_col(slots), by_col(slots)],
+        out_specs=[pl.BlockSpec((2, slots, cut), lambda n: (0, 0, n)), whole((slots, 1))] + [whole((slots, wide))] * PARTS,
         grid=(3,),
+        scratch=[pltpu.VMEM((slots, width), BF)],
         flops=2 * slots * width * ff,
-    )
+        limit=MOST,
+    )
+    grads, score, h_far = lax.optimization_barrier((grads, score, h_far))
     g_left, g_right = go_up(grads), go_down(grads)
     by_row = pl.BlockSpec((wide, ff), lambda q: (q, 0))
     back = call(
@@ -345,10 +342,12 @@
         grid=(PARTS,),
         scratch=[pltpu.VMEM((slots, width), BF)],
         flops=4 * slots * width * ff,
+        limit=MOST,
     )[0]
     back_rows = exchange(back)
-    s_far = go_up(s_left[slots:]), go_down(s_right[slots:])
+    g_left, g_right, s_next, s_across, s_last = lax.optimization_barrier((g_left, g_right, s_next, s_across, s_last))
     g_far = go_up(g_left[0]), go_down(g_right[1])
+    s_left, s_right, s_far = go_up(s_next), go_down(s_last), go_across(s_across)
     grad_tokens, grad_gates_t = call(
         functools.partial(finish_kernel, owners, cap),
         [shape((toks, width)), shape((top, toks))],
@@ -359,16 +358,16 @@
 
     partial = call(
         near_kernel,
-        [shape((wide, ff), F32), shape((wide, ff), F32), shape((ff, wide), F32)],
-        [x_own, s_own, hidden, grads, x_left, s_left, h_left, g_left, x_right, s_right, h_right, g_right],
-        flops=HINT * 6 * 3 * slots * wide * ff,
+        [shape((wide, ff), F32), shape((wide, ff), F32)],
+        [x_own, grads, x_left, g_left, x_right, g_right],
+        flops=HINT * 4 * 3 * slots * wide * ff,
         limit=MOST,
     )
     grad_gate, grad_up, grad_down = call(
-        far_kernel,
+        last_kernel,
         [shape((wide, ff)), shape((wide, ff)), shape((ff, wide))],
-        [*x_far, *s_far, *h_far, *g_far, *partial],
-        flops=HINT * 6 * slots * wide * ff,
+        [x_far, *g_far, *partial, hidden, s_own, h_left, s_left, h_right, s_right, *h_far, s_far],
+        flops=HINT * 12 * slots * wide * ff,
         limit=MOST,
     )
     return grad_tokens, grad_gates_t.T, grad_gate[None], grad_up[None], grad_down[None]

time: 188 us -> 186 us (0.989); the launches traced: 187 us -> 182 us
  local copies, waits for them, and re-layouts: 15.5 us -> 5.73 us
  Pallas kernels: 36.7 us -> 44.9 us
  starting transfers between devices: 47.5 us -> 43.3 us
    ppermute x8 -> x6, waiting for transfers between devices: 23.6 us -> 4.91 us  [go_down(): return lax.ppermute(v, 'dp', [(i, (i - 1) % groups) for i in range(groups)])]
    all_to_all x3, waiting for transfers between devices: 39.1 us -> 57.7 us  [exchange(): v = lax.all_to_all(v, 'expert', split_axis=0, concat_axis=0, tiled=True)]
    unnamed x66 -> x34, local copies, waits for them, and re-layouts: 13.2 us -> 4.45 us
    pallas_call x10 -> x9, Pallas kernels: 36.7 us -> 44.9 us  [call(): pl.pallas_call(kernel, out_shape=outs, grid=grid, in_specs=specs or [whol...]
    ppermute x8 -> x6, starting transfers between devices: 11.6 us -> 6.24 us  [go_down(): return lax.ppermute(v, 'dp', [(i, (i - 1) % groups) for i in range(groups)])]
    ppermute x8 -> x6, waiting for transfers between devices: 24.1 us -> 24.9 us  [go_up(): return lax.ppermute(v, 'dp', [(i, (i + 1) % groups) for i in range(groups)])]
    ppermute x8 -> x6, starting transfers between devices: 7.72 us -> 7.53 us  [go_up(): return lax.ppermute(v, 'dp', [(i, (i + 1) % groups) for i in range(groups)])]
  transfers between devices with their start and end apart: 19 -> 17, of which waited for: 12 -> 9; matrix products, arithmetic and copies ran while one was open for 1% -> 1% of each run, Pallas kernels for 15% -> 22%
where the time goes in v1:
time: 186 us; the launch traced here: 182 us
  waiting for transfers between devices  87.5 us (47%)
  Pallas kernels  44.9 us (24%)
  starting transfers between devices  43.3 us (23%)
  local copies, waits for them, and re-layouts  5.73 us (3%)
    all_to_all x3, waiting for transfers between devices, exchange(): v = lax.all_to_all(v, 'expert', split_axis=0, concat_axis=0, tiled=True)  57.7 us
    pallas_call x9, Pallas kernels, call(): pl.pallas_call(kernel, out_shape=outs, grid=grid, in_specs=specs or [whol...  44.9 us
    all_to_all x3, starting transfers between devices, exchange(): v = lax.all_to_all(v, 'expert', split_axis=0, concat_axis=0, tiled=True)  28.4 us
    ppermute x6, waiting for transfers between devices, go_up(): return lax.ppermute(v, 'dp', [(i, (i + 1) % groups) for i in range(groups)])  24.9 us
    ppermute x6, starting transfers between devices, go_up(): return lax.ppermute(v, 'dp', [(i, (i + 1) % groups) for i in range(groups)])  7.53 us
    ppermute x6, starting transfers between devices, go_down(): return lax.ppermute(v, 'dp', [(i, (i - 1) % groups) for i in range(groups)])  6.24 us
    ppermute x6, waiting for transfers between devices, go_down(): return lax.ppermute(v, 'dp', [(i, (i - 1) % groups) for i in range(groups)])  4.91 us
    unnamed x34, local copies, waits for them, and re-layouts  4.45 us
  transfers between devices with their start and end apart: 17, of which 9 were waited for; matrix products, arithmetic and copies ran while one was open for 1% of the time, Pallas kernels for 22%

profile of v1, /device:TPU:6, one launch (start us, length us, event | category | flops | bytes accessed | tf_op | source)
XLA Modules:
  0.0 182.3 jit_solution(16955971608776950835)
XLA Ops:
  0.6 3.4 %shard_map.129 = bf16[1536,512]{1,0:T(8,128)(2,1)} custom-call(s32[2,128]{1,0:T(2,128)} %bitcast.22, bf16[2,128]{1,0:T(2,128)(2,1)} %bitcast.25, bf16[128,2048]{1,0:T(8,128)(2,1)} %x_ref.3, bf16[192,192]{1,0:T(8,128)(2,1)} %constant.10.clone.packer_ref), custom_call_target="tpu_custom_call" | custom-call | flops 201326592 | bytes 2172416 | tf_op jit(solution)/shard_map/pallas_call | solution.py:40
  4.1 12.1 %all-to-all-start.1 = ((bf16[64,24,512]{2,1,0:T(8,128)(2,1)}), bf16[64,24,512]{2,1,0:T(8,128)(2,1)S(1)}, u32[]{:S(2)}, u32[]{:S(2)}) async-start(bf16[64,24,512]{2,1,0:T(8,128)(2,1)} %bitcast.30), calls=%async_computation.1 | async-start | bytes 3145728 | tf_op jit(solution)/shard_map/all_to_all | solution.py:278
  16.2 3.5 %shard_map.128 = bf16[1536,512]{1,0:T(8,128)(2,1)} custom-call(s32[2,128]{1,0:T(2,128)} %bitcast.23, bf16[2,128]{1,0:T(2,128)(2,1)} %bitcast.26, bf16[128,2048]{1,0:T(8,128)(2,1)} %x_ref.2, bf16[192,192]{1,0:T(8,128)(2,1)} %constant.10.clone.packer_ref), custom_call_target="tpu_custom_call" | custom-call | flops 201326592 | bytes 2172416 | tf_op jit(solution)/shard_map/pallas_call | solution.py:40
  19.7 36.6 %all-to-all-done.1 = bf16[64,24,512]{2,1,0:T(8,128)(2,1)S(1)} async-done(((bf16[64,24,512]{2,1,0:T(8,128)(2,1)}), bf16[64,24,512]{2,1,0:T(8,128)(2,1)S(1)}, u32[]{:S(2)}, u32[]{:S(2)}) %all-to-all-start.1) | async-done | bytes 1572896 | tf_op jit(solution)/shard_map/all_to_all | solution.py:278
  56.3 5.7 %all-to-all-start = ((bf16[64,24,512]{2,1,0:T(8,128)(2,1)}), bf16[64,24,512]{2,1,0:T(8,128)(2,1)}, u32[]{:S(2)}, u32[]{:S(2)}) async-start(bf16[64,24,512]{2,1,0:T(8,128)(2,1)} %bitcast.29), calls=%async_computation | async-start | bytes 3145728 | tf_op jit(solution)/shard_map/all_to_all | solution.py:278
  62.7 1.1 copy-done.4
  63.8 0.7 copy-done.5
  65.0 1.5 collective-permute-start.2
  66.6 6.9 %shard_map.131 = (f32[384,768]{1,0:T(8,128)}, f32[384,768]{1,0:T(8,128)}, bf16[384,768]{1,0:T(8,128)(2,1)}) custom-call(bf16[384,2048]{1,0:T(8,128)(2,1)} %copy-done.4, bf16[2048,768]{1,0:T(8,128)(2,1)} %bitcast.32, bf16[2048,768]{1,0:T(8,128)(2,1)} %bitcast.34), custom_call_target="tpu_custom_call" | custom-call | flops 2415919104 | bytes 10813440 | tf_op jit(solution)/shard_map/pallas_call | solution.py:40
  73.5 2.0 %collective-permute-done.1.refs_2_ = bf16[384,512]{1,0:T(8,128)(2,1)S(1)} collective-permute-done((bf16[384,512]{1,0:T(8,128)(2,1)S(1)}, bf16[384,512]{1,0:T(8,128)(2,1)S(1)}, u32[]{:S(2)}, u32[]{:S(2)}) %collective-permute-start.1) | collective-permute-done | bytes 393248 | tf_op jit(solution)/shard_map/ppermute | solution.py:268
  75.6 1.4 collective-permute-done.2.refs_4_
  77.0 0.8 copy-done.13
  78.2 1.6 collective-permute-start.4
  79.8 1.2 collective-permute-start
  81.0 21.0 %all-to-all-done = bf16[64,24,512]{2,1,0:T(8,128)(2,1)} async-done(((bf16[64,24,512]{2,1,0:T(8,128)(2,1)}), bf16[64,24,512]{2,1,0:T(8,128)(2,1)}, u32[]{:S(2)}, u32[]{:S(2)}) %all-to-all-start) | async-done | bytes 1572896 | tf_op jit(solution)/shard_map/all_to_all | solution.py:278
  102.2 1.1 collective-permute-start.5
  103.4 1.1 collective-permute-start.6
  104.4 7.2 %shard_map.132 = (bf16[2,384,768]{2,1,0:T(8,128)(2,1)}, f32[384,1]{1,0:T(8,128)}, bf16[384,512]{1,0:T(8,128)(2,1)}, bf16[384,512]{1,0:T(8,128)(2,1)}, bf16[384,5...) custom-call(s32[1]{0:T(128)} %bitcast.2.pos_ref, bf16[1536,512]{1,0:T(8,128)(2,1)} %bitcast.4.in_ref, ...), custom_call_target="tpu_custom_call" | custom-call | flops 1207959552 | bytes 9905668 | tf_op jit(solution)/shard_map/pallas_call | solution.py:40
  111.7 0.7 copy-done.15
  112.5 2.3 %collective-permute-start.7 = (bf16[2,384,768]{2,1,0:T(8,128)(2,1)}, bf16[2,384,768]{2,1,0:T(8,128)(2,1)S(1)}, u32[]{:S(2)}, u32[]{:S(2)}) collective-permute-start(bf16[2,384,768]{2,1,0:T(8,128)(2,1)} %get-tuple-element.55.g_ref.refs_1_), channel_id=1, source_target_pairs={{0,64},{64,128},{128,192},{192,0},{1,65},{65,129},{129,193},{193,1... | collective-permute-start | bytes 3538952 | tf_op jit(solution)/shard_map/ppermute | solution.py:268
  114.8 7.9 %shard_map.133 = bf16[512,1664]{1,0:T(8,128)(2,1)} custom-call(bf16[2,384,768]{2,1,0:T(8,128)(2,1)} %get-tuple-element.55.g_ref.refs_1_, bf16[2048,768]{1,0:T(8,128)(2,1)} %bitcast.33, bf16[2048,768]{1,0:T(8,128)(2,1)} %bitcast.35, f32[384,1]{1,0:T(8,128)} %get-tuple-element.56.score_ref, bf16[192,192]{1,0:T(8,128)(2,1)} %constant.11.clone.liner_ref), custom_call_target="tpu_custom_call" | custom-call | flops 2415919104 | bytes 9250304 | tf_op jit(solution)/shard_map/pallas_call | solution.py:40
  122.7 10.6 %all-to-all-start.2 = ((bf16[64,8,1664]{2,1,0:T(8,128)(2,1)}), bf16[64,8,1664]{2,1,0:T(8,128)(2,1)S(1)}, u32[]{:S(2)}, u32[]{:S(2)}) async-start(bf16[64,8,1664]{2,1,0:T(8,128)(2,1)} %bitcast.28), calls=%async_computation.2 | async-start | bytes 3407872 | tf_op jit(solution)/shard_map/all_to_all | solution.py:278
  133.2 5.6 %collective-permute-done.7.refs_3_ = bf16[2,384,768]{2,1,0:T(8,128)(2,1)S(1)} collective-permute-done((bf16[2,384,768]{2,1,0:T(8,128)(2,1)}, bf16[2,384,768]{2,1,0:T(8,128)(2,1)S(1)}, u32[]{:S(2)}, u32[]{:S(2)}) %collective-permute-start.7) | collective-permute-done | bytes 1179680 | tf_op jit(solution)/shard_map/ppermute | solution.py:268
  138.8 2.7 %collective-permute-done.8.refs_5_ = bf16[2,384,768]{2,1,0:T(8,128)(2,1)} collective-permute-done((bf16[2,384,768]{2,1,0:T(8,128)(2,1)}, bf16[2,384,768]{2,1,0:T(8,128)(2,1)}, u32[]{:S(2)}, u32[]{:S(2)}) %collective-permute-start.8) | collective-permute-done | bytes 1179680 | tf_op jit(solution)/shard_map/ppermute | solution.py:274
  141.5 1.2 slice_bitcast_fusion
  143.0 3.1 %collective-permute-start.9 = (bf16[384,768]{1,0:T(8,128)(2,1)S(1)}, bf16[384,768]{1,0:T(8,128)(2,1)}, u32[]{:S(2)}, u32[]{:S(2)}) collective-permute-start(bf16[384,768]{1,0:T(8,128)(2,1)S(1)} %slice_bitcast_fusion.1), channel_id=1, source_target_pairs={{0,64},{64,128},{128,192},{192,0},{1,65},{65,129},{129,193},{193,1... | collective-permute-start | bytes 1769480 | tf_op jit(solution)/shard_map/ppermute | solution.py:268
  146.3 1.9 %collective-permute-start.12 = (bf16[384,512]{1,0:T(8,128)(2,1)}, bf16[384,512]{1,0:T(8,128)(2,1)}, u32[]{:S(2)}, u32[]{:S(2)}) collective-permute-start(bf16[384,512]{1,0:T(8,128)(2,1)} %get-tuple-element.72), channel_id=1, source_target_pairs={{0,192},{64,0},{128,64},{192,128},{1,193},{65,1},{129,65},{193,129... | collective-permute-start | bytes 1179656 | tf_op jit(solution)/shard_map/ppermute | solution.py:274
  148.2 6.5 %shard_map.135 = (f32[512,768]{1,0:T(8,128)}, f32[512,768]{1,0:T(8,128)}) custom-call(bf16[384,512]{1,0:T(8,128)(2,1)} %copy-done.5, bf16[2,384,768]{2,1,0:T(8,128)(2,1)} %get-tuple-element.55.g_ref.refs_1_, bf16[384,512]{1,0:T(8,128)(2,1)} %copy-done.12, bf16[2,384,768]{2,1,0:T(8,128)(2,1)} %copy-done.6, bf16[384,512]{1,0:T(8,128)(2,1)} %copy-done.13, ...), custom_call_target="tpu_custom_call" | custom-call | flops 18119393280 | bytes 7864320 | tf_op jit(solution)/shard_map/pallas_call | solution.py:40
  154.8 17.3 %collective-permute-done.11.refs_3_ = bf16[384,512]{1,0:T(8,128)(2,1)S(1)} collective-permute-done((bf16[384,512]{1,0:T(8,128)(2,1)}, bf16[384,512]{1,0:T(8,128)(2,1)S(1)}, u32[]{:S(2)}, u32[]{:S(2)}) %collective-permute-start.11) | collective-permute-done | bytes 393248 | tf_op jit(solution)/shard_map/ppermute | solution.py:268
  172.8 0.7 copy-done.10
  173.5 7.0 %shard_map.136 = (bf16[512,768]{1,0:T(8,128)(2,1)}, bf16[512,768]{1,0:T(8,128)(2,1)}, bf16[768,512]{1,0:T(8,128)(2,1)}) custom-call(bf16[384,512]{1,0:T(8,128)(2,1)} %copy-done.11, bf16[384,768]{1,0:T(8,128)(2,1)} %collective-permute-done.9.g0, bf16[384,768]{1,0:T(8,128)(2,1)} %copy-done.10, f32[512,768]{1,0:T(8,128)} %get-tuple-element.68.pgate, ...), custom_call_target="tpu_custom_call" | custom-call | flops 18119393280 | bytes 11010048 | tf_op jit(solution)/shard_map/pallas_call | solution.py:40
  180.5 1.8 shard_map.134
  (49 shorter events, 3.1 us)
Async XLA Ops:
  4.1 52.2 %all-to-all-start.1 = ((bf16[64,24,512]{2,1,0:T(8,128)(2,1)}), bf16[64,24,512]{2,1,0:T(8,128)(2,1)S(1)}, u32[]{:S(2)}, u32[]{:S(2)}) async-start(bf16[64,24,512]{2,1,0:T(8,128)(2,1)} %bitcast.30), calls=%async_computation.1 | async-start | bytes 3145728 | tf_op jit(solution)/shard_map/all_to_all | solution.py:278
  56.3 5.7 %copy-start = (bf16[192,192]{1,0:T(8,128)(2,1)S(1)}, bf16[192,192]{1,0:T(8,128)(2,1)}, u32[]{:S(2)}) copy-start(bf16[192,192]{1,0:T(8,128)(2,1)} %constant.10.clone.packer_ref) | copy-start | bytes 221188
  56.3 45.7 %all-to-all-start = ((bf16[64,24,512]{2,1,0:T(8,128)(2,1)}), bf16[64,24,512]{2,1,0:T(8,128)(2,1)}, u32[]{:S(2)}, u32[]{:S(2)}) async-start(bf16[64,24,512]{2,1,0:T(8,128)(2,1)} %bitcast.29), calls=%async_computation | async-start | bytes 3145728 | tf_op jit(solution)/shard_map/all_to_all | solution.py:278
  62.7 1.1 copy-start.4
  63.8 0.7 copy-start.5
  64.6 11.0 %collective-permute-start.1 = (bf16[384,512]{1,0:T(8,128)(2,1)S(1)}, bf16[384,512]{1,0:T(8,128)(2,1)S(1)}, u32[]{:S(2)}, u32[]{:S(2)}) collective-permute-start(bf16[384,512]{1,0:T(8,128)(2,1)S(1)} %get-tuple-element.45), channel_id=1, source_target_pairs={{0,64},{64,128},{128,192},{192,0},{1,65},{65,129},{129,193},{193,1... | collective-permute-start | bytes 1179656 | tf_op jit(solution)/shard_map/ppermute | solution.py:268
  65.0 11.9 %collective-permute-start.2 = (bf16[384,512]{1,0:T(8,128)(2,1)S(1)}, bf16[384,512]{1,0:T(8,128)(2,1)S(1)}, u32[]{:S(2)}, u32[]{:S(2)}) collective-permute-start(bf16[384,512]{1,0:T(8,128)(2,1)S(1)} %get-tuple-element.46), channel_id=1, source_target_pairs={{0,192},{64,0},{128,64},{192,128},{1,193},{65,1},{129,65},{193,129... | collective-permute-start | bytes 1179656 | tf_op jit(solution)/shard_map/ppermute | solution.py:274
  75.6 1.4 copy-start.12
  77.0 0.8 copy-start.13
  77.8 24.3 %collective-permute-start.3 = (bf16[384,768]{1,0:T(8,128)(2,1)}, bf16[384,768]{1,0:T(8,128)(2,1)S(1)}, u32[]{:S(2)}, u32[]{:S(2)}) collective-permute-start(bf16[384,768]{1,0:T(8,128)(2,1)} %get-tuple-element.47.refs_0_), channel_id=1, source_target_pairs={{0,64},{64,128},{128,192},{192,0},{1,65},{65,129},{129,193},{193,1... | collective-permute-start | bytes 1769480 | tf_op jit(solution)/shard_map/ppermute | solution.py:268
  78.2 24.1 %collective-permute-start.4 = (bf16[384,768]{1,0:T(8,128)(2,1)}, bf16[384,768]{1,0:T(8,128)(2,1)S(1)}, u32[]{:S(2)}, u32[]{:S(2)}) collective-permute-start(bf16[384,768]{1,0:T(8,128)(2,1)} %get-tuple-element.47.refs_0_), channel_id=1, source_target_pairs={{0,192},{64,0},{128,64},{192,128},{1,193},{65,1},{129,65},{193,129... | collective-permute-start | bytes 1769480 | tf_op jit(solution)/shard_map/ppermute | solution.py:274
  79.8 22.2 %collective-permute-start = (bf16[384,512]{1,0:T(8,128)(2,1)S(1)}, bf16[384,512]{1,0:T(8,128)(2,1)S(1)}, u32[]{:S(2)}, u32[]{:S(2)}) collective-permute-start(bf16[384,512]{1,0:T(8,128)(2,1)S(1)} %get-tuple-element.42), channel_id=1, source_target_pairs={{0,128},{64,192},{128,0},{192,64},{1,129},{65,193},{129,1},{193,65... | collective-permute-start | bytes 1179656 | tf_op jit(solution)/shard_map/ppermute | solution.py:271
  102.0 9.6 %copy-start.11 = (bf16[384,512]{1,0:T(8,128)(2,1)}, bf16[384,512]{1,0:T(8,128)(2,1)S(1)}, u32[]{:S(2)}) copy-start(bf16[384,512]{1,0:T(8,128)(2,1)S(1)} %collective-permute-done.x) | copy-start | bytes 1179652
  102.0 9.6 %copy-start.8 = (bf16[384,768]{1,0:T(8,128)(2,1)}, bf16[384,768]{1,0:T(8,128)(2,1)S(1)}, u32[]{:S(2)}) copy-start(bf16[384,768]{1,0:T(8,128)(2,1)S(1)} %collective-permute-done.3.refs_2_) | copy-start | bytes 1769476
  102.2 9.5 %copy-start.9 = (bf16[384,768]{1,0:T(8,128)(2,1)}, bf16[384,768]{1,0:T(8,128)(2,1)S(1)}, u32[]{:S(2)}) copy-start(bf16[384,768]{1,0:T(8,128)(2,1)S(1)} %collective-permute-done.4.refs_4_) | copy-start | bytes 1769476
  102.2 9.4 %collective-permute-start.5 = (bf16[192,768]{1,0:T(8,128)(2,1)S(1)}, bf16[192,768]{1,0:T(8,128)(2,1)S(1)}, u32[]{:S(2)}, u32[]{:S(2)}) collective-permute-start(bf16[192,768]{1,0:T(8,128)(2,1)S(1)} %slice.12), channel_id=1, source_target_pairs={{0,64},{64,128},{128,192},{192,0},{1,65},{65,129},{129,193},{193,1... | collective-permute-start | bytes 884744 | tf_op jit(solution)/shard_map/ppermute | solution.py:268
  103.4 8.3 %collective-permute-start.6 = (bf16[192,768]{1,0:T(8,128)(2,1)S(1)}, bf16[192,768]{1,0:T(8,128)(2,1)S(1)}, u32[]{:S(2)}, u32[]{:S(2)}) collective-permute-start(bf16[192,768]{1,0:T(8,128)(2,1)S(1)} %slice.13), channel_id=1, source_target_pairs={{0,192},{64,0},{128,64},{192,128},{1,193},{65,1},{129,65},{193,129... | collective-permute-start | bytes 884744 | tf_op jit(solution)/shard_map/ppermute | solution.py:274
  111.7 0.8 copy-start.16
  112.5 26.3 %collective-permute-start.7 = (bf16[2,384,768]{2,1,0:T(8,128)(2,1)}, bf16[2,384,768]{2,1,0:T(8,128)(2,1)S(1)}, u32[]{:S(2)}, u32[]{:S(2)}) collective-permute-start(bf16[2,384,768]{2,1,0:T(8,128)(2,1)} %get-tuple-element.55.g_ref.refs_1_), channel_id=1, source_target_pairs={{0,64},{64,128},{128,192},{192,0},{1,65},{65,129},{129,193},{193,1... | collective-permute-start | bytes 3538952 | tf_op jit(solution)/shard_map/ppermute | solution.py:268
  114.8 26.8 %collective-permute-start.8 = (bf16[2,384,768]{2,1,0:T(8,128)(2,1)}, bf16[2,384,768]{2,1,0:T(8,128)(2,1)}, u32[]{:S(2)}, u32[]{:S(2)}) collective-permute-start(bf16[2,384,768]{2,1,0:T(8,128)(2,1)} %get-tuple-element.55.g_ref.refs_1_), channel_id=1, source_target_pairs={{0,192},{64,0},{128,64},{192,128},{1,193},{65,1},{129,65},{193,129... | collective-permute-start | bytes 3538952 | tf_op jit(solution)/shard_map/ppermute | solution.py:274
  122.7 57.8 %all-to-all-start.2 = ((bf16[64,8,1664]{2,1,0:T(8,128)(2,1)}), bf16[64,8,1664]{2,1,0:T(8,128)(2,1)S(1)}, u32[]{:S(2)}, u32[]{:S(2)}) async-start(bf16[64,8,1664]{2,1,0:T(8,128)(2,1)} %bitcast.28), calls=%async_computation.2 | async-start | bytes 3407872 | tf_op jit(solution)/shard_map/all_to_all | solution.py:278
  138.8 2.7 %copy-start.6 = (bf16[2,384,768]{2,1,0:T(8,128)(2,1)}, bf16[2,384,768]{2,1,0:T(8,128)(2,1)S(1)}, u32[]{:S(2)}) copy-start(bf16[2,384,768]{2,1,0:T(8,128)(2,1)S(1)} %collective-permute-done.7.refs_3_) | copy-start | bytes 3538948
  141.5 1.4 copy-start.7
  142.7 29.9 %collective-permute-start.10 = (bf16[384,768]{1,0:T(8,128)(2,1)S(1)}, bf16[384,768]{1,0:T(8,128)(2,1)S(1)}, u32[]{:S(2)}, u32[]{:S(2)}) collective-permute-start(bf16[384,768]{1,0:T(8,128)(2,1)S(1)} %slice_bitcast_fusion), channel_id=1, source_target_pairs={{0,192},{64,0},{128,64},{192,128},{1,193},{65,1},{129,65},{193,129... | collective-permute-start | bytes 1769480 | tf_op jit(solution)/shard_map/ppermute | solution.py:274
  143.0 29.6 %collective-permute-start.9 = (bf16[384,768]{1,0:T(8,128)(2,1)S(1)}, bf16[384,768]{1,0:T(8,128)(2,1)}, u32[]{:S(2)}, u32[]{:S(2)}) collective-permute-start(bf16[384,768]{1,0:T(8,128)(2,1)S(1)} %slice_bitcast_fusion.1), channel_id=1, source_target_pairs={{0,64},{64,128},{128,192},{192,0},{1,65},{65,129},{129,193},{193,1... | collective-permute-start | bytes 1769480 | tf_op jit(solution)/shard_map/ppermute | solution.py:268
  146.2 25.9 %collective-permute-start.11 = (bf16[384,512]{1,0:T(8,128)(2,1)}, bf16[384,512]{1,0:T(8,128)(2,1)S(1)}, u32[]{:S(2)}, u32[]{:S(2)}) collective-permute-start(bf16[384,512]{1,0:T(8,128)(2,1)} %get-tuple-element.71), channel_id=1, source_target_pairs={{0,64},{64,128},{128,192},{192,0},{1,65},{65,129},{129,193},{193,1... | collective-permute-start | bytes 1179656 | tf_op jit(solution)/shard_map/ppermute | solution.py:268
  146.3 26.4 %collective-permute-start.12 = (bf16[384,512]{1,0:T(8,128)(2,1)}, bf16[384,512]{1,0:T(8,128)(2,1)}, u32[]{:S(2)}, u32[]{:S(2)}) collective-permute-start(bf16[384,512]{1,0:T(8,128)(2,1)} %get-tuple-element.72), channel_id=1, source_target_pairs={{0,192},{64,0},{128,64},{192,128},{1,193},{65,1},{129,65},{193,129... | collective-permute-start | bytes 1179656 | tf_op jit(solution)/shard_map/ppermute | solution.py:274
  148.2 24.4 %collective-permute-start.13 = (bf16[384,512]{1,0:T(8,128)(2,1)}, bf16[384,512]{1,0:T(8,128)(2,1)}, u32[]{:S(2)}, u32[]{:S(2)}) collective-permute-start(bf16[384,512]{1,0:T(8,128)(2,1)} %get-tuple-element.75), channel_id=1, source_target_pairs={{0,128},{64,192},{128,0},{192,64},{1,129},{65,193},{129,1},{193,65... | collective-permute-start | bytes 1179656 | tf_op jit(solution)/shard_map/ppermute | solution.py:271
  172.7 0.8 copy-start.10
  173.5 7.0 %copy-start.1 = (bf16[192,192]{1,0:T(8,128)(2,1)S(1)}, bf16[192,192]{1,0:T(8,128)(2,1)}, u32[]{:S(2)}) copy-start(bf16[192,192]{1,0:T(8,128)(2,1)} %constant.11.clone.liner_ref) | copy-start | bytes 221188
  173.5 7.0 %copy-start.2 = (s32[128,2]{0,1:T(2,128)S(1)}, s32[128,2]{0,1:T(2,128)}, u32[]{:S(2)}) copy-start(s32[128,2]{0,1:T(2,128)} %param.10) | copy-start | bytes 3076
  173.5 7.0 %copy-start.3 = (bf16[128,2]{0,1:T(2,128)(2,1)S(1)}, bf16[128,2]{0,1:T(2,128)(2,1)}, u32[]{:S(2)}) copy-start(bf16[128,2]{0,1:T(2,128)(2,1)} %param.11) | copy-start | bytes 1540
  (2 other events, 1.4 us)

commit v2 on v1

--- a/solution.py
+++ b/solution.py
@@ -232,19 +232,23 @@
         gg_ref[k : k + 1, :] = (value / gates_ref[k : k + 1, :].astype(F32)).astype(BF)
 
 
-def near_kernel(*refs):
-    ins, outs = refs[:-2], refs[-2:]
-    for k, out in enumerate(outs):
+def near_kernel(far_ref, *refs):
+    ins, (gate, up, turned) = refs[:-3], refs[-3:]
+    turned[...] = far_ref[...].T
+    for k, out in enumerate((gate, up)):
         out[...] = sum(t_dot(x[...], g[k]) for x, g in zip(ins[::2], ins[1::2]))
 
 
-def last_kernel(x, g0, g1, pgate, pup, *refs):
-    near, (ha, hb, s), (gate, up, down) = refs[:-6], refs[-6:-3], refs[-3:]
+def down_kernel(*refs):
+    near, (ha, hb, s, down) = refs[:-4], refs[-4:]
     half = ha.shape[0]
-    gate[...] = (pgate[...] + t_dot(x[...], g0[...])).astype(BF)
-    up[...] = (pup[...] + t_dot(x[...], g1[...])).astype(BF)
     far = t_dot(ha[...], s[:half, :]) + t_dot(hb[...], s[half:, :])
     down[...] = (sum(t_dot(h[...], v[...]) for h, v in zip(near[::2], near[1::2])) + far).astype(BF)
+
+
+def last_kernel(x, g0, g1, pgate, pup, gate, up):
+    gate[...] = (pgate[...] + dot(x[...], g0[...])).astype(BF)
+    up[...] = (pup[...] + dot(x[...], g1[...])).astype(BF)
 
 
 def body(tokens, expert_ids, gates, cotangent, w_gate, w_up, w_down):
@@ -346,8 +350,11 @@
     )[0]
     back_rows = exchange(back)
     g_left, g_right, s_next, s_across, s_last = lax.optimization_barrier((g_left, g_right, s_next, s_across, s_last))
-    g_far = go_up(g_left[0]), go_down(g_right[1])
     s_left, s_right, s_far = go_up(s_next), go_down(s_last), go_across(s_across)
+    g_first, g_second, s_left, s_right, s_far = lax.optimization_barrier(
+        (g_left[0], g_right[1], s_left, s_right, s_far)
+    )
+    g_first, g_second = go_up(g_first), go_down(g_second)
     grad_tokens, grad_gates_t = call(
         functools.partial(finish_kernel, owners, cap),
         [shape((toks, width)), shape((top, toks))],
@@ -356,18 +363,28 @@
         flops=2 * slots * toks * width,
     )
 
-    partial = call(
+    *partial, x_turned = call(
         near_kernel,
-        [shape((wide, ff), F32), shape((wide, ff), F32)],
-        [x_own, grads, x_left, g_left, x_right, g_right],
+        [shape((wide, ff), F32), shape((wide, ff), F32), shape((wide, slots))],
+        [x_far, x_own, grads, x_left, g_left, x_right, g_right],
         flops=HINT * 4 * 3 * slots * wide * ff,
         limit=MOST,
     )
-    grad_gate, grad_up, grad_down = call(
+    grad_down = call(
+        down_kernel,
+        [shape((ff, wide))],
+        [hidden, s_own, h_left, s_left, h_right, s_right, *h_far, s_far],
+        flops=HINT * 8 * slots * wide * ff,
+        limit=MOST,
+    )[0]
+    grad_gate, grad_up = call(
         last_kernel,
-        [shape((wide, ff)), shape((wide, ff)), shape((ff, wide))],
-        [x_far, *g_far, *partial, hidden, s_own, h_left, s_left, h_right, s_right, *h_far, s_far],
-        flops=HINT * 12 * slots * wide * ff,
+        [shape((wide, ff)), shape((wide, ff))],
+        [x_turned, g_first, g_second, *partial],
+        specs=[whole(x_turned.shape), by_col(slots), by_col(slots), by_col(wide), by_col(wide)],
+        out_specs=[by_col(wide), by_col(wide)],
+        grid=(3,),
+        flops=HINT * 4 * slots * wide * ff,
         limit=MOST,
     )
     return grad_tokens, grad_gates_t.T, grad_gate[None], grad_up[None], grad_down[None]

time: 186 us -> 186 us (level)
  Pallas kernels: 44.9 us -> 48 us
    ppermute x6, waiting for transfers between devices: 24.9 us -> 15.6 us  [go_up(): return lax.ppermute(v, 'dp', [(i, (i + 1) % groups) for i in range(groups)])]
    ppermute x6, waiting for transfers between devices: 4.91 us -> 13.8 us  [go_down(): return lax.ppermute(v, 'dp', [(i, (i - 1) % groups) for i in range(groups)])]
    pallas_call x9 -> x10, Pallas kernels: 44.9 us -> 48 us  [call(): pl.pallas_call(kernel, out_shape=outs, grid=grid, in_specs=specs or [whol...]
    ppermute x6, starting transfers between devices: 6.24 us -> 4.23 us  [go_down(): return lax.ppermute(v, 'dp', [(i, (i - 1) % groups) for i in range(groups)])]
  transfers between devices with their start and end apart: 17 -> 17, of which waited for: 9 -> 11; matrix products, arithmetic and copies ran while one was open for 1% -> 1% of each run, Pallas kernels for 22% -> 23%
where the time goes in v2:
time: 186 us; the launch traced here: 184 us
  waiting for transfers between devices  87.1 us (47%)
  Pallas kernels  48 us (26%)
  starting transfers between devices  43.9 us (24%)
  local copies, waits for them, and re-layouts  4.06 us (2%)
    all_to_all x3, waiting for transfers between devices, exchange(): v = lax.all_to_all(v, 'expert', split_axis=0, concat_axis=0, tiled=True)  57.7 us
    pallas_call x10, Pallas kernels, call(): pl.pallas_call(kernel, out_shape=outs, grid=grid, in_specs=specs or [whol...  48 us
    all_to_all x3, starting transfers between devices, exchange(): v = lax.all_to_all(v, 'expert', split_axis=0, concat_axis=0, tiled=True)  28.5 us
    ppermute x6, waiting for transfers between devices, go_up(): return lax.ppermute(v, 'dp', [(i, (i + 1) % groups) for i in range(groups)])  15.6 us
    ppermute x6, waiting for transfers between devices, go_down(): return lax.ppermute(v, 'dp', [(i, (i - 1) % groups) for i in range(groups)])  13.8 us
    ppermute x6, starting transfers between devices, go_up(): return lax.ppermute(v, 'dp', [(i, (i + 1) % groups) for i in range(groups)])  8.26 us
    ppermute x6, starting transfers between devices, go_down(): return lax.ppermute(v, 'dp', [(i, (i - 1) % groups) for i in range(groups)])  4.23 us
  transfers between devices with their start and end apart: 17, of which 11 were waited for; matrix products, arithmetic and copies ran while one was open for 1% of the time, Pallas kernels for 23%

profile of v2, /device:TPU:6, one launch (start us, length us, event | category | flops | bytes accessed | tf_op | source)
XLA Modules:
  0.0 183.9 jit_solution(626612940932326203)
XLA Ops:
  0.6 3.4 %shard_map.129 = bf16[1536,512]{1,0:T(8,128)(2,1)} custom-call(s32[2,128]{1,0:T(2,128)} %bitcast.22, bf16[2,128]{1,0:T(2,128)(2,1)} %bitcast.25, bf16[128,2048]{1,0:T(8,128)(2,1)} %x_ref.3, bf16[192,192]{1,0:T(8,128)(2,1)} %constant.10.clone.packer_ref), custom_call_target="tpu_custom_call" | custom-call | flops 201326592 | bytes 2172416 | tf_op jit(solution)/shard_map/pallas_call | solution.py:40
  4.1 12.1 %all-to-all-start.1 = ((bf16[64,24,512]{2,1,0:T(8,128)(2,1)}), bf16[64,24,512]{2,1,0:T(8,128)(2,1)S(1)}, u32[]{:S(2)}, u32[]{:S(2)}) async-start(bf16[64,24,512]{2,1,0:T(8,128)(2,1)} %bitcast.30), calls=%async_computation.1 | async-start | bytes 3145728 | tf_op jit(solution)/shard_map/all_to_all | solution.py:282
  16.2 3.5 %shard_map.128 = bf16[1536,512]{1,0:T(8,128)(2,1)} custom-call(s32[2,128]{1,0:T(2,128)} %bitcast.23, bf16[2,128]{1,0:T(2,128)(2,1)} %bitcast.26, bf16[128,2048]{1,0:T(8,128)(2,1)} %x_ref.2, bf16[192,192]{1,0:T(8,128)(2,1)} %constant.10.clone.packer_ref), custom_call_target="tpu_custom_call" | custom-call | flops 201326592 | bytes 2172416 | tf_op jit(solution)/shard_map/pallas_call | solution.py:40
  19.7 36.6 %all-to-all-done.1 = bf16[64,24,512]{2,1,0:T(8,128)(2,1)S(1)} async-done(((bf16[64,24,512]{2,1,0:T(8,128)(2,1)}), bf16[64,24,512]{2,1,0:T(8,128)(2,1)S(1)}, u32[]{:S(2)}, u32[]{:S(2)}) %all-to-all-start.1) | async-done | bytes 1572896 | tf_op jit(solution)/shard_map/all_to_all | solution.py:282
  56.3 5.7 %all-to-all-start = ((bf16[64,24,512]{2,1,0:T(8,128)(2,1)}), bf16[64,24,512]{2,1,0:T(8,128)(2,1)}, u32[]{:S(2)}, u32[]{:S(2)}) async-start(bf16[64,24,512]{2,1,0:T(8,128)(2,1)} %bitcast.29), calls=%async_computation | async-start | bytes 3145728 | tf_op jit(solution)/shard_map/all_to_all | solution.py:282
  62.7 1.1 copy-done.4
  65.1 1.5 collective-permute-start.2
  66.6 6.9 %shard_map.131 = (f32[384,768]{1,0:T(8,128)}, f32[384,768]{1,0:T(8,128)}, bf16[384,768]{1,0:T(8,128)(2,1)}) custom-call(bf16[384,2048]{1,0:T(8,128)(2,1)} %copy-done.4, bf16[2048,768]{1,0:T(8,128)(2,1)} %bitcast.32, bf16[2048,768]{1,0:T(8,128)(2,1)} %bitcast.34), custom_call_target="tpu_custom_call" | custom-call | flops 2415919104 | bytes 10813440 | tf_op jit(solution)/shard_map/pallas_call | solution.py:40
  73.5 2.1 %collective-permute-done.1.refs_2_ = bf16[384,512]{1,0:T(8,128)(2,1)S(1)} collective-permute-done((bf16[384,512]{1,0:T(8,128)(2,1)S(1)}, bf16[384,512]{1,0:T(8,128)(2,1)S(1)}, u32[]{:S(2)}, u32[]{:S(2)}) %collective-permute-start.1) | collective-permute-done | bytes 393248 | tf_op jit(solution)/shard_map/ppermute | solution.py:272
  75.6 1.4 collective-permute-done.2.refs_4_
  78.2 1.6 collective-permute-start.4
  79.8 1.2 collective-permute-start
  81.0 21.0 %all-to-all-done = bf16[64,24,512]{2,1,0:T(8,128)(2,1)} async-done(((bf16[64,24,512]{2,1,0:T(8,128)(2,1)}), bf16[64,24,512]{2,1,0:T(8,128)(2,1)}, u32[]{:S(2)}, u32[]{:S(2)}) %all-to-all-start) | async-done | bytes 1572896 | tf_op jit(solution)/shard_map/all_to_all | solution.py:282
  102.2 1.1 collective-permute-start.5
  103.4 1.1 collective-permute-start.6
  104.4 7.2 %shard_map.132 = (bf16[2,384,768]{2,1,0:T(8,128)(2,1)}, f32[384,1]{1,0:T(8,128)}, bf16[384,512]{1,0:T(8,128)(2,1)}, bf16[384,512]{1,0:T(8,128)(2,1)}, bf16[384,5...) custom-call(s32[1]{0:T(128)} %bitcast.2.pos_ref, bf16[1536,512]{1,0:T(8,128)(2,1)} %bitcast.4.in_ref, ...), custom_call_target="tpu_custom_call" | custom-call | flops 1207959552 | bytes 9905668 | tf_op jit(solution)/shard_map/pallas_call | solution.py:40
  111.7 2.5 %collective-permute-start.7 = (bf16[2,384,768]{2,1,0:T(8,128)(2,1)}, bf16[2,384,768]{2,1,0:T(8,128)(2,1)S(1)}, u32[]{:S(2)}, u32[]{:S(2)}) collective-permute-start(bf16[2,384,768]{2,1,0:T(8,128)(2,1)} %get-tuple-element.60.g_ref.refs_1_), channel_id=1, source_target_pairs={{0,64},{64,128},{128,192},{192,0},{1,65},{65,129},{129,193},{193,1... | collective-permute-start | bytes 3538952 | tf_op jit(solution)/shard_map/ppermute | solution.py:272
  114.2 7.9 %shard_map.133 = bf16[512,1664]{1,0:T(8,128)(2,1)} custom-call(bf16[2,384,768]{2,1,0:T(8,128)(2,1)} %get-tuple-element.60.g_ref.refs_1_, bf16[2048,768]{1,0:T(8,128)(2,1)} %bitcast.33, bf16[2048,768]{1,0:T(8,128)(2,1)} %bitcast.35, f32[384,1]{1,0:T(8,128)} %get-tuple-element.61.score_ref, bf16[192,192]{1,0:T(8,128)(2,1)} %constant.11.clone.liner_ref), custom_call_target="tpu_custom_call" | custom-call | flops 2415919104 | bytes 9250304 | tf_op jit(solution)/shard_map/pallas_call | solution.py:40
  122.1 10.7 %all-to-all-start.2 = ((bf16[64,8,1664]{2,1,0:T(8,128)(2,1)}), bf16[64,8,1664]{2,1,0:T(8,128)(2,1)S(1)}, u32[]{:S(2)}, u32[]{:S(2)}) async-start(bf16[64,8,1664]{2,1,0:T(8,128)(2,1)} %bitcast.28), calls=%async_computation.2 | async-start | bytes 3407872 | tf_op jit(solution)/shard_map/all_to_all | solution.py:282
  132.9 5.4 %collective-permute-done.7.refs_3_ = bf16[2,384,768]{2,1,0:T(8,128)(2,1)S(1)} collective-permute-done((bf16[2,384,768]{2,1,0:T(8,128)(2,1)}, bf16[2,384,768]{2,1,0:T(8,128)(2,1)S(1)}, u32[]{:S(2)}, u32[]{:S(2)}) %collective-permute-start.7) | collective-permute-done | bytes 1179680 | tf_op jit(solution)/shard_map/ppermute | solution.py:272
  138.3 2.7 %collective-permute-done.8.refs_5_ = bf16[2,384,768]{2,1,0:T(8,128)(2,1)} collective-permute-done((bf16[2,384,768]{2,1,0:T(8,128)(2,1)}, bf16[2,384,768]{2,1,0:T(8,128)(2,1)}, u32[]{:S(2)}, u32[]{:S(2)}) %collective-permute-start.8) | collective-permute-done | bytes 1179680 | tf_op jit(solution)/shard_map/ppermute | solution.py:278
  141.0 1.6 collective-permute-start.11
  142.6 1.6 collective-permute-start.9
  144.2 6.7 %shard_map.135 = (f32[512,768]{1,0:T(8,128)}, f32[512,768]{1,0:T(8,128)}, bf16[512,384]{1,0:T(8,128)(2,1)}) custom-call(bf16[384,512]{1,0:T(8,128)(2,1)} %copy-done.12, bf16[384,512]{1,0:T(8,128)(2,1)} %copy-done.5, bf16[2,384,768]{2,1,0:T(8,128)(2,1)} %get-tuple-element.60.g_ref.refs_1_, bf16[384,512]{1,0:T(8,128)(2,1)} %copy-done.10, ...), custom_call_target="tpu_custom_call" | custom-call | flops 18119393280 | bytes 8650752 | tf_op jit(solution)/shard_map/pallas_call | solution.py:40
  151.0 1.3 slice_bitcast_fusion
  152.3 6.0 %collective-permute-done.10.refs_5_ = bf16[384,512]{1,0:T(8,128)(2,1)S(1)} collective-permute-done((bf16[384,512]{1,0:T(8,128)(2,1)}, bf16[384,512]{1,0:T(8,128)(2,1)S(1)}, u32[]{:S(2)}, u32[]{:S(2)}) %collective-permute-start.10) | collective-permute-done | bytes 393248 | tf_op jit(solution)/shard_map/ppermute | solution.py:278
  159.0 2.1 %collective-permute-start.12 = (bf16[384,768]{1,0:T(8,128)(2,1)S(1)}, bf16[384,768]{1,0:T(8,128)(2,1)S(1)}, u32[]{:S(2)}, u32[]{:S(2)}) collective-permute-start(bf16[384,768]{1,0:T(8,128)(2,1)S(1)} %get-tuple-element.77), channel_id=1, source_target_pairs={{0,64},{64,128},{128,192},{192,0},{1,65},{65,129},{129,193},{193,1... | collective-permute-start | bytes 1769480 | tf_op jit(solution)/shard_map/ppermute | solution.py:272
  161.2 4.8 %shard_map.137 = bf16[768,512]{1,0:T(8,128)(2,1)} custom-call(bf16[384,768]{1,0:T(8,128)(2,1)} %get-tuple-element.52.refs_0_, bf16[384,512]{1,0:T(8,128)(2,1)} %get-tuple-element.83.refs_1_, bf16[384,768]{1,0:T(8,128)(2,1)} %copy-done.7, bf16[384,512]{1,0:T(8,128)(2,1)} %collective-permute-done.9.refs_3_, bf16[384,768]{1,0:T(8,128)(2,1)} %copy-done.8, ...), custom_call_target="tpu_custom_call" | custom-call | flops 12079595520 | bytes 4718592 | tf_op jit(solution)/shard_map/pallas_call | solution.py:40
  165.9 7.4 %collective-permute-done.12.g0 = bf16[384,768]{1,0:T(8,128)(2,1)S(1)} collective-permute-done((bf16[384,768]{1,0:T(8,128)(2,1)S(1)}, bf16[384,768]{1,0:T(8,128)(2,1)S(1)}, u32[]{:S(2)}, u32[]{:S(2)}) %collective-permute-start.12) | collective-permute-done | bytes 589856 | tf_op jit(solution)/shard_map/ppermute | solution.py:272
  173.4 3.5 %collective-permute-done.13.g1 = bf16[384,768]{1,0:T(8,128)(2,1)} collective-permute-done((bf16[384,768]{1,0:T(8,128)(2,1)S(1)}, bf16[384,768]{1,0:T(8,128)(2,1)}, u32[]{:S(2)}, u32[]{:S(2)}) %collective-permute-start.13) | collective-permute-done | bytes 589856 | tf_op jit(solution)/shard_map/ppermute | solution.py:278
  176.9 5.2 %shard_map.136 = (bf16[512,768]{1,0:T(8,128)(2,1)}, bf16[512,768]{1,0:T(8,128)(2,1)}) custom-call(bf16[512,384]{1,0:T(8,128)(2,1)} %get-tuple-element.73.x, bf16[384,768]{1,0:T(8,128)(2,1)} %copy-done.9, bf16[384,768]{1,0:T(8,128)(2,1)} %collective-permute-done.13.g1, f32[512,768]{1,0:T(8,128)} %get-tuple-element.79.pgate, f32[512,768]{1,0:T(8,128)} %get-tuple-element.80.pup), custom_call_target="tpu_custom_call" | custom-call | flops 6039797760 | bytes 6291456 | tf_op jit(solution)/shard_map/pallas_call | solution.py:40
  182.1 1.8 shard_map.134
  (49 shorter events, 4.1 us)
Async XLA Ops:
  4.1 52.2 %all-to-all-start.1 = ((bf16[64,24,512]{2,1,0:T(8,128)(2,1)}), bf16[64,24,512]{2,1,0:T(8,128)(2,1)S(1)}, u32[]{:S(2)}, u32[]{:S(2)}) async-start(bf16[64,24,512]{2,1,0:T(8,128)(2,1)} %bitcast.30), calls=%async_computation.1 | async-start | bytes 3145728 | tf_op jit(solution)/shard_map/all_to_all | solution.py:282
  56.3 5.7 %copy-start = (bf16[192,192]{1,0:T(8,128)(2,1)S(1)}, bf16[192,192]{1,0:T(8,128)(2,1)}, u32[]{:S(2)}) copy-start(bf16[192,192]{1,0:T(8,128)(2,1)} %constant.10.clone.packer_ref) | copy-start | bytes 221188
  56.3 45.7 %all-to-all-start = ((bf16[64,24,512]{2,1,0:T(8,128)(2,1)}), bf16[64,24,512]{2,1,0:T(8,128)(2,1)}, u32[]{:S(2)}, u32[]{:S(2)}) async-start(bf16[64,24,512]{2,1,0:T(8,128)(2,1)} %bitcast.29), calls=%async_computation | async-start | bytes 3145728 | tf_op jit(solution)/shard_map/all_to_all | solution.py:282
  62.7 1.1 copy-start.4
  64.6 11.0 %collective-permute-start.1 = (bf16[384,512]{1,0:T(8,128)(2,1)S(1)}, bf16[384,512]{1,0:T(8,128)(2,1)S(1)}, u32[]{:S(2)}, u32[]{:S(2)}) collective-permute-start(bf16[384,512]{1,0:T(8,128)(2,1)S(1)} %get-tuple-element.50), channel_id=1, source_target_pairs={{0,64},{64,128},{128,192},{192,0},{1,65},{65,129},{129,193},{193,1... | collective-permute-start | bytes 1179656 | tf_op jit(solution)/shard_map/ppermute | solution.py:272
  65.1 11.9 %collective-permute-start.2 = (bf16[384,512]{1,0:T(8,128)(2,1)S(1)}, bf16[384,512]{1,0:T(8,128)(2,1)S(1)}, u32[]{:S(2)}, u32[]{:S(2)}) collective-permute-start(bf16[384,512]{1,0:T(8,128)(2,1)S(1)} %get-tuple-element.51), channel_id=1, source_target_pairs={{0,192},{64,0},{128,64},{192,128},{1,193},{65,1},{129,65},{193,129... | collective-permute-start | bytes 1179656 | tf_op jit(solution)/shard_map/ppermute | solution.py:278
  75.6 1.4 copy-start.10
  77.8 24.3 %collective-permute-start.3 = (bf16[384,768]{1,0:T(8,128)(2,1)}, bf16[384,768]{1,0:T(8,128)(2,1)S(1)}, u32[]{:S(2)}, u32[]{:S(2)}) collective-permute-start(bf16[384,768]{1,0:T(8,128)(2,1)} %get-tuple-element.52.refs_0_), channel_id=1, source_target_pairs={{0,64},{64,128},{128,192},{192,0},{1,65},{65,129},{129,193},{193,1... | collective-permute-start | bytes 1769480 | tf_op jit(solution)/shard_map/ppermute | solution.py:272
  78.2 24.0 %collective-permute-start.4 = (bf16[384,768]{1,0:T(8,128)(2,1)}, bf16[384,768]{1,0:T(8,128)(2,1)S(1)}, u32[]{:S(2)}, u32[]{:S(2)}) collective-permute-start(bf16[384,768]{1,0:T(8,128)(2,1)} %get-tuple-element.52.refs_0_), channel_id=1, source_target_pairs={{0,192},{64,0},{128,64},{192,128},{1,193},{65,1},{129,65},{193,129... | collective-permute-start | bytes 1769480 | tf_op jit(solution)/shard_map/ppermute | solution.py:278
  79.8 22.2 %collective-permute-start = (bf16[384,512]{1,0:T(8,128)(2,1)S(1)}, bf16[384,512]{1,0:T(8,128)(2,1)S(1)}, u32[]{:S(2)}, u32[]{:S(2)}) collective-permute-start(bf16[384,512]{1,0:T(8,128)(2,1)S(1)} %get-tuple-element.47), channel_id=1, source_target_pairs={{0,128},{64,192},{128,0},{192,64},{1,129},{65,193},{129,1},{193,65... | collective-permute-start | bytes 1179656 | tf_op jit(solution)/shard_map/ppermute | solution.py:275
  102.0 9.6 %copy-start.12 = (bf16[384,512]{1,0:T(8,128)(2,1)}, bf16[384,512]{1,0:T(8,128)(2,1)S(1)}, u32[]{:S(2)}) copy-start(bf16[384,512]{1,0:T(8,128)(2,1)S(1)} %collective-permute-done.far_ref) | copy-start | bytes 1179652
  102.0 9.6 %copy-start.7 = (bf16[384,768]{1,0:T(8,128)(2,1)}, bf16[384,768]{1,0:T(8,128)(2,1)S(1)}, u32[]{:S(2)}) copy-start(bf16[384,768]{1,0:T(8,128)(2,1)S(1)} %collective-permute-done.3.refs_2_) | copy-start | bytes 1769476
  102.2 9.5 %copy-start.8 = (bf16[384,768]{1,0:T(8,128)(2,1)}, bf16[384,768]{1,0:T(8,128)(2,1)S(1)}, u32[]{:S(2)}) copy-start(bf16[384,768]{1,0:T(8,128)(2,1)S(1)} %collective-permute-done.4.refs_4_) | copy-start | bytes 1769476
  102.2 9.4 %collective-permute-start.5 = (bf16[192,768]{1,0:T(8,128)(2,1)S(1)}, bf16[192,768]{1,0:T(8,128)(2,1)S(1)}, u32[]{:S(2)}, u32[]{:S(2)}) collective-permute-start(bf16[192,768]{1,0:T(8,128)(2,1)S(1)} %slice.12), channel_id=1, source_target_pairs={{0,64},{64,128},{128,192},{192,0},{1,65},{65,129},{129,193},{193,1... | collective-permute-start | bytes 884744 | tf_op jit(solution)/shard_map/ppermute | solution.py:272
  103.4 8.3 %collective-permute-start.6 = (bf16[192,768]{1,0:T(8,128)(2,1)S(1)}, bf16[192,768]{1,0:T(8,128)(2,1)S(1)}, u32[]{:S(2)}, u32[]{:S(2)}) collective-permute-start(bf16[192,768]{1,0:T(8,128)(2,1)S(1)} %slice.13), channel_id=1, source_target_pairs={{0,192},{64,0},{128,64},{192,128},{1,193},{65,1},{129,65},{193,129... | collective-permute-start | bytes 884744 | tf_op jit(solution)/shard_map/ppermute | solution.py:278
  111.7 10.4 %copy-start.15 = (bf16[192,768]{1,0:T(8,128)(2,1)}, bf16[192,768]{1,0:T(8,128)(2,1)S(1)}, u32[]{:S(2)}) copy-start(bf16[192,768]{1,0:T(8,128)(2,1)S(1)} %collective-permute-done.5.refs_6_) | copy-start | bytes 884740
  111.7 10.4 %copy-start.16 = (bf16[192,768]{1,0:T(8,128)(2,1)}, bf16[192,768]{1,0:T(8,128)(2,1)S(1)}, u32[]{:S(2)}) copy-start(bf16[192,768]{1,0:T(8,128)(2,1)S(1)} %collective-permute-done.6.refs_7_) | copy-start | bytes 884740
  111.7 26.6 %collective-permute-start.7 = (bf16[2,384,768]{2,1,0:T(8,128)(2,1)}, bf16[2,384,768]{2,1,0:T(8,128)(2,1)S(1)}, u32[]{:S(2)}, u32[]{:S(2)}) collective-permute-start(bf16[2,384,768]{2,1,0:T(8,128)(2,1)} %get-tuple-element.60.g_ref.refs_1_), channel_id=1, source_target_pairs={{0,64},{64,128},{128,192},{192,0},{1,65},{65,129},{129,193},{193,1... | collective-permute-start | bytes 3538952 | tf_op jit(solution)/shard_map/ppermute | solution.py:272
  114.2 26.8 %collective-permute-start.8 = (bf16[2,384,768]{2,1,0:T(8,128)(2,1)}, bf16[2,384,768]{2,1,0:T(8,128)(2,1)}, u32[]{:S(2)}, u32[]{:S(2)}) collective-permute-start(bf16[2,384,768]{2,1,0:T(8,128)(2,1)} %get-tuple-element.60.g_ref.refs_1_), channel_id=1, source_target_pairs={{0,192},{64,0},{128,64},{192,128},{1,193},{65,1},{129,65},{193,129... | collective-permute-start | bytes 3538952 | tf_op jit(solution)/shard_map/ppermute | solution.py:278
  122.1 20.5 %copy-start.13 = (bf16[384,512]{1,0:T(8,128)(2,1)S(1)}, bf16[384,512]{1,0:T(8,128)(2,1)}, u32[]{:S(2)}) copy-start(bf16[384,512]{1,0:T(8,128)(2,1)} %get-tuple-element.74) | copy-start | bytes 1179652
  122.1 60.0 %all-to-all-start.2 = ((bf16[64,8,1664]{2,1,0:T(8,128)(2,1)}), bf16[64,8,1664]{2,1,0:T(8,128)(2,1)S(1)}, u32[]{:S(2)}, u32[]{:S(2)}) async-start(bf16[64,8,1664]{2,1,0:T(8,128)(2,1)} %bitcast.28), calls=%async_computation.2 | async-start | bytes 3407872 | tf_op jit(solution)/shard_map/all_to_all | solution.py:282
  138.3 6.0 %copy-start.6 = (bf16[2,384,768]{2,1,0:T(8,128)(2,1)}, bf16[2,384,768]{2,1,0:T(8,128)(2,1)S(1)}, u32[]{:S(2)}) copy-start(bf16[2,384,768]{2,1,0:T(8,128)(2,1)S(1)} %collective-permute-done.7.refs_3_) | copy-start | bytes 3538948
  141.0 17.3 %collective-permute-start.10 = (bf16[384,512]{1,0:T(8,128)(2,1)}, bf16[384,512]{1,0:T(8,128)(2,1)S(1)}, u32[]{:S(2)}, u32[]{:S(2)}) collective-permute-start(bf16[384,512]{1,0:T(8,128)(2,1)} %get-tuple-element.75), channel_id=1, source_target_pairs={{0,192},{64,0},{128,64},{192,128},{1,193},{65,1},{129,65},{193,129... | collective-permute-start | bytes 1179656 | tf_op jit(solution)/shard_map/ppermute | solution.py:278
  141.0 17.3 %collective-permute-start.11 = (bf16[384,512]{1,0:T(8,128)(2,1)}, bf16[384,512]{1,0:T(8,128)(2,1)}, u32[]{:S(2)}, u32[]{:S(2)}) collective-permute-start(bf16[384,512]{1,0:T(8,128)(2,1)} %get-tuple-element.76), channel_id=1, source_target_pairs={{0,128},{64,192},{128,0},{192,64},{1,129},{65,193},{129,1},{193,65... | collective-permute-start | bytes 1179656 | tf_op jit(solution)/shard_map/ppermute | solution.py:275
  142.6 16.4 %collective-permute-start.9 = (bf16[384,512]{1,0:T(8,128)(2,1)S(1)}, bf16[384,512]{1,0:T(8,128)(2,1)}, u32[]{:S(2)}, u32[]{:S(2)}) collective-permute-start(bf16[384,512]{1,0:T(8,128)(2,1)S(1)} %copy-done.13), channel_id=1, source_target_pairs={{0,64},{64,128},{128,192},{192,0},{1,65},{65,129},{129,193},{193,1... | collective-permute-start | bytes 1179656 | tf_op jit(solution)/shard_map/ppermute | solution.py:272
  158.3 2.9 %copy-start.14 = (bf16[384,512]{1,0:T(8,128)(2,1)}, bf16[384,512]{1,0:T(8,128)(2,1)S(1)}, u32[]{:S(2)}) copy-start(bf16[384,512]{1,0:T(8,128)(2,1)S(1)} %collective-permute-done.10.refs_5_) | copy-start | bytes 1179652
  159.0 14.3 %collective-permute-start.12 = (bf16[384,768]{1,0:T(8,128)(2,1)S(1)}, bf16[384,768]{1,0:T(8,128)(2,1)S(1)}, u32[]{:S(2)}, u32[]{:S(2)}) collective-permute-start(bf16[384,768]{1,0:T(8,128)(2,1)S(1)} %get-tuple-element.77), channel_id=1, source_target_pairs={{0,64},{64,128},{128,192},{192,0},{1,65},{65,129},{129,193},{193,1... | collective-permute-start | bytes 1769480 | tf_op jit(solution)/shard_map/ppermute | solution.py:272
  161.2 15.7 %collective-permute-start.13 = (bf16[384,768]{1,0:T(8,128)(2,1)S(1)}, bf16[384,768]{1,0:T(8,128)(2,1)}, u32[]{:S(2)}, u32[]{:S(2)}) collective-permute-start(bf16[384,768]{1,0:T(8,128)(2,1)S(1)} %get-tuple-element.78), channel_id=1, source_target_pairs={{0,192},{64,0},{128,64},{192,128},{1,193},{65,1},{129,65},{193,129... | collective-permute-start | bytes 1769480 | tf_op jit(solution)/shard_map/ppermute | solution.py:278
  173.4 3.5 %copy-start.9 = (bf16[384,768]{1,0:T(8,128)(2,1)}, bf16[384,768]{1,0:T(8,128)(2,1)S(1)}, u32[]{:S(2)}) copy-start(bf16[384,768]{1,0:T(8,128)(2,1)S(1)} %collective-permute-done.12.g0) | copy-start | bytes 1769476
  176.9 5.2 %copy-start.1 = (bf16[192,192]{1,0:T(8,128)(2,1)S(1)}, bf16[192,192]{1,0:T(8,128)(2,1)}, u32[]{:S(2)}) copy-start(bf16[192,192]{1,0:T(8,128)(2,1)} %constant.11.clone.liner_ref) | copy-start | bytes 221188
  176.9 5.2 %copy-start.2 = (s32[128,2]{0,1:T(2,128)S(1)}, s32[128,2]{0,1:T(2,128)}, u32[]{:S(2)}) copy-start(s32[128,2]{0,1:T(2,128)} %param.10) | copy-start | bytes 3076
  176.9 5.2 %copy-start.3 = (bf16[128,2]{0,1:T(2,128)(2,1)S(1)}, bf16[128,2]{0,1:T(2,128)(2,1)}, u32[]{:S(2)}) copy-start(bf16[128,2]{0,1:T(2,128)(2,1)} %param.11) | copy-start | bytes 1540
  (2 other events, 1.5 us)

commit v3 on v2

--- a/solution.py
+++ b/solution.py
@@ -16,6 +16,7 @@
 GROUP = 8
 LIMIT = 40 * 1024 * 1024
 MOST = 60 * 1024 * 1024
+SMALL = 24 * 1024 * 1024
 SM = pl.BlockSpec(memory_space=pltpu.SMEM)
 
 
@@ -368,14 +369,14 @@
         [shape((wide, ff), F32), shape((wide, ff), F32), shape((wide, slots))],
         [x_far, x_own, grads, x_left, g_left, x_right, g_right],
         flops=HINT * 4 * 3 * slots * wide * ff,
-        limit=MOST,
+        limit=SMALL,
     )
     grad_down = call(
         down_kernel,
         [shape((ff, wide))],
         [hidden, s_own, h_left, s_left, h_right, s_right, *h_far, s_far],
         flops=HINT * 8 * slots * wide * ff,
-        limit=MOST,
+        limit=SMALL,
     )[0]
     grad_gate, grad_up = call(
         last_kernel,
@@ -385,7 +386,7 @@
         out_specs=[by_col(wide), by_col(wide)],
         grid=(3,),
         flops=HINT * 4 * slots * wide * ff,
-        limit=MOST,
+        limit=SMALL,
     )
     return grad_tokens, grad_gates_t.T, grad_gate[None], grad_up[None], grad_down[None]
 

time: 186 us -> 183 us (0.984)
  Pallas kernels: 48 us -> 41 us
  local copies, waits for them, and re-layouts: 4.06 us -> 8.97 us
    pallas_call x10, Pallas kernels: 48 us -> 41 us  [call(): pl.pallas_call(kernel, out_shape=outs, grid=grid, in_specs=specs or [whol...]
    unnamed x34 -> x44, local copies, waits for them, and re-layouts: 2.7 us -> 7.47 us
    ppermute x6, waiting for transfers between devices: 13.8 us -> 11.8 us  [go_down(): return lax.ppermute(v, 'dp', [(i, (i - 1) % groups) for i in range(groups)])]
  transfers between devices with their start and end apart: 17 -> 17, of which waited for: 11 -> 11; matrix products, arithmetic and copies ran while one was open for 1% -> 1% of each run, Pallas kernels for 23% -> 20%
where the time goes in v3:
time: 183 us; the launch traced here: 181 us
  waiting for transfers between devices  86.6 us (47%)
  starting transfers between devices  43.8 us (24%)
  Pallas kernels  41 us (22%)
  local copies, waits for them, and re-layouts  8.97 us (5%)
    all_to_all x3, waiting for transfers between devices, exchange(): v = lax.all_to_all(v, 'expert', split_axis=0, concat_axis=0, tiled=True)  57.6 us
    pallas_call x10, Pallas kernels, call(): pl.pallas_call(kernel, out_shape=outs, grid=grid, in_specs=specs or [whol...  41 us
    all_to_all x3, starting transfers between devices, exchange(): v = lax.all_to_all(v, 'expert', split_axis=0, concat_axis=0, tiled=True)  28.5 us
    ppermute x6, waiting for transfers between devices, go_up(): return lax.ppermute(v, 'dp', [(i, (i + 1) % groups) for i in range(groups)])  17.2 us
    ppermute x6, waiting for transfers between devices, go_down(): return lax.ppermute(v, 'dp', [(i, (i - 1) % groups) for i in range(groups)])  11.8 us
    ppermute x6, starting transfers between devices, go_up(): return lax.ppermute(v, 'dp', [(i, (i + 1) % groups) for i in range(groups)])  7.71 us
    unnamed x44, local copies, waits for them, and re-layouts  7.47 us
    ppermute x6, starting transfers between devices, go_down(): return lax.ppermute(v, 'dp', [(i, (i - 1) % groups) for i in range(groups)])  4.65 us
  transfers between devices with their start and end apart: 17, of which 11 were waited for; matrix products, arithmetic and copies ran while one was open for 1% of the time, Pallas kernels for 20%

profile of v3, /device:TPU:6, one launch (start us, length us, event | category | flops | bytes accessed | tf_op | source)
XLA Modules:
  0.0 181.3 jit_solution(18431517301698409115)
XLA Ops:
  0.6 3.4 %shard_map.129 = bf16[1536,512]{1,0:T(8,128)(2,1)} custom-call(s32[2,128]{1,0:T(2,128)} %bitcast.22, bf16[2,128]{1,0:T(2,128)(2,1)} %bitcast.25, bf16[128,2048]{1,0:T(8,128)(2,1)} %x_ref.3, bf16[192,192]{1,0:T(8,128)(2,1)} %constant.10.clone.packer_ref), custom_call_target="tpu_custom_call" | custom-call | flops 201326592 | bytes 2172416 | tf_op jit(solution)/shard_map/pallas_call | solution.py:41
  4.1 12.1 %all-to-all-start.1 = ((bf16[64,24,512]{2,1,0:T(8,128)(2,1)}), bf16[64,24,512]{2,1,0:T(8,128)(2,1)S(1)}, u32[]{:S(2)}, u32[]{:S(2)}) async-start(bf16[64,24,512]{2,1,0:T(8,128)(2,1)} %bitcast.30), calls=%async_computation.1 | async-start | bytes 3145728 | tf_op jit(solution)/shard_map/all_to_all | solution.py:283
  16.2 3.5 %shard_map.128 = bf16[1536,512]{1,0:T(8,128)(2,1)} custom-call(s32[2,128]{1,0:T(2,128)} %bitcast.23, bf16[2,128]{1,0:T(2,128)(2,1)} %bitcast.26, bf16[128,2048]{1,0:T(8,128)(2,1)} %x_ref.2, bf16[192,192]{1,0:T(8,128)(2,1)} %constant.10.clone.packer_ref), custom_call_target="tpu_custom_call" | custom-call | flops 201326592 | bytes 2172416 | tf_op jit(solution)/shard_map/pallas_call | solution.py:41
  19.7 36.6 %all-to-all-done.1 = bf16[64,24,512]{2,1,0:T(8,128)(2,1)S(1)} async-done(((bf16[64,24,512]{2,1,0:T(8,128)(2,1)}), bf16[64,24,512]{2,1,0:T(8,128)(2,1)S(1)}, u32[]{:S(2)}, u32[]{:S(2)}) %all-to-all-start.1) | async-done | bytes 1572896 | tf_op jit(solution)/shard_map/all_to_all | solution.py:283
  56.3 5.7 %all-to-all-start = ((bf16[64,24,512]{2,1,0:T(8,128)(2,1)}), bf16[64,24,512]{2,1,0:T(8,128)(2,1)}, u32[]{:S(2)}, u32[]{:S(2)}) async-start(bf16[64,24,512]{2,1,0:T(8,128)(2,1)} %bitcast.29), calls=%async_computation | async-start | bytes 3145728 | tf_op jit(solution)/shard_map/all_to_all | solution.py:283
  62.7 1.2 copy-done.7
  65.1 1.5 collective-permute-start.2
  66.6 6.9 %shard_map.131 = (f32[384,768]{1,0:T(8,128)}, f32[384,768]{1,0:T(8,128)}, bf16[384,768]{1,0:T(8,128)(2,1)}) custom-call(bf16[384,2048]{1,0:T(8,128)(2,1)} %copy-done.7, bf16[2048,768]{1,0:T(8,128)(2,1)} %bitcast.32, bf16[2048,768]{1,0:T(8,128)(2,1)} %bitcast.34), custom_call_target="tpu_custom_call" | custom-call | flops 2415919104 | bytes 10813440 | tf_op jit(solution)/shard_map/pallas_call | solution.py:41
  73.6 2.1 %collective-permute-done.1.refs_2_ = bf16[384,512]{1,0:T(8,128)(2,1)S(1)} collective-permute-done((bf16[384,512]{1,0:T(8,128)(2,1)S(1)}, bf16[384,512]{1,0:T(8,128)(2,1)S(1)}, u32[]{:S(2)}, u32[]{:S(2)}) %collective-permute-start.1) | collective-permute-done | bytes 393248 | tf_op jit(solution)/shard_map/ppermute | solution.py:273
  77.8 1.1 collective-permute-start.3
  79.8 1.2 collective-permute-start
  81.0 21.0 %all-to-all-done = bf16[64,24,512]{2,1,0:T(8,128)(2,1)} async-done(((bf16[64,24,512]{2,1,0:T(8,128)(2,1)}), bf16[64,24,512]{2,1,0:T(8,128)(2,1)}, u32[]{:S(2)}, u32[]{:S(2)}) %all-to-all-start) | async-done | bytes 1572896 | tf_op jit(solution)/shard_map/all_to_all | solution.py:283
  103.4 1.7 collective-permute-start.6
  105.1 7.2 %shard_map.132 = (bf16[2,384,768]{2,1,0:T(8,128)(2,1)}, f32[384,1]{1,0:T(8,128)}, bf16[384,512]{1,0:T(8,128)(2,1)}, bf16[384,512]{1,0:T(8,128)(2,1)}, bf16[384,5...) custom-call(s32[1]{0:T(128)} %bitcast.2.pos_ref, bf16[1536,512]{1,0:T(8,128)(2,1)} %bitcast.4.in_ref, ...), custom_call_target="tpu_custom_call" | custom-call | flops 1207959552 | bytes 9905668 | tf_op jit(solution)/shard_map/pallas_call | solution.py:41
  112.4 1.9 %collective-permute-start.7 = (bf16[2,384,768]{2,1,0:T(8,128)(2,1)}, bf16[2,384,768]{2,1,0:T(8,128)(2,1)}, u32[]{:S(2)}, u32[]{:S(2)}) collective-permute-start(bf16[2,384,768]{2,1,0:T(8,128)(2,1)} %get-tuple-element.60.g_ref.refs_1_), channel_id=1, source_target_pairs={{0,64},{64,128},{128,192},{192,0},{1,65},{65,129},{129,193},{193,1... | collective-permute-start | bytes 3538952 | tf_op jit(solution)/shard_map/ppermute | solution.py:273
  114.6 7.9 %shard_map.133 = bf16[512,1664]{1,0:T(8,128)(2,1)} custom-call(bf16[2,384,768]{2,1,0:T(8,128)(2,1)} %get-tuple-element.60.g_ref.refs_1_, bf16[2048,768]{1,0:T(8,128)(2,1)} %bitcast.33, bf16[2048,768]{1,0:T(8,128)(2,1)} %bitcast.35, f32[384,1]{1,0:T(8,128)} %get-tuple-element.61.score_ref, bf16[192,192]{1,0:T(8,128)(2,1)} %constant.11.clone.liner_ref), custom_call_target="tpu_custom_call" | custom-call | flops 2415919104 | bytes 9250304 | tf_op jit(solution)/shard_map/pallas_call | solution.py:41
  122.5 10.7 %all-to-all-start.2 = ((bf16[64,8,1664]{2,1,0:T(8,128)(2,1)}), bf16[64,8,1664]{2,1,0:T(8,128)(2,1)S(1)}, u32[]{:S(2)}, u32[]{:S(2)}) async-start(bf16[64,8,1664]{2,1,0:T(8,128)(2,1)} %bitcast.28), calls=%async_computation.2 | async-start | bytes 3407872 | tf_op jit(solution)/shard_map/all_to_all | solution.py:283
  133.3 5.1 %collective-permute-done.7.refs_3_ = bf16[2,384,768]{2,1,0:T(8,128)(2,1)} collective-permute-done((bf16[2,384,768]{2,1,0:T(8,128)(2,1)}, bf16[2,384,768]{2,1,0:T(8,128)(2,1)}, u32[]{:S(2)}, u32[]{:S(2)}) %collective-permute-start.7) | collective-permute-done | bytes 1179680 | tf_op jit(solution)/shard_map/ppermute | solution.py:273
  138.4 2.6 %collective-permute-done.8.refs_5_ = bf16[2,384,768]{2,1,0:T(8,128)(2,1)} collective-permute-done((bf16[2,384,768]{2,1,0:T(8,128)(2,1)}, bf16[2,384,768]{2,1,0:T(8,128)(2,1)}, u32[]{:S(2)}, u32[]{:S(2)}) %collective-permute-start.8) | collective-permute-done | bytes 1179680 | tf_op jit(solution)/shard_map/ppermute | solution.py:279
  141.0 1.7 collective-permute-start.11
  142.7 1.5 collective-permute-start.9
  144.2 1.0 copy-done.10
  145.2 1.0 copy-done.12
  148.2 4.3 %shard_map.135 = (f32[512,768]{1,0:T(8,128)S(1)}, f32[512,768]{1,0:T(8,128)S(1)}, bf16[512,384]{1,0:T(8,128)(2,1)S(1)}) custom-call(bf16[384,512]{1,0:T(8,128)(2,1)S(1)} %copy-done.17, bf16[384,512]{1,0:T(8,128)(2,1)S(1)} %copy-done.10, bf16[2,384,768]{2,1,0:T(8,128)(2,1)S(1)} %copy-done.1, bf16[384,512]{1,0:T(8,128)(2,1)S(1)} %copy-done.12, ...), custom_call_target="tpu_custom_call" | custom-call | flops 18119393280 | bytes 8650752 | tf_op jit(solution)/shard_map/pallas_call | solution.py:41
  152.5 1.5 slice_bitcast_fusion
  154.0 4.3 %collective-permute-done.10.refs_5_ = bf16[384,512]{1,0:T(8,128)(2,1)S(1)} collective-permute-done((bf16[384,512]{1,0:T(8,128)(2,1)}, bf16[384,512]{1,0:T(8,128)(2,1)S(1)}, u32[]{:S(2)}, u32[]{:S(2)}) %collective-permute-start.10) | collective-permute-done | bytes 393248 | tf_op jit(solution)/shard_map/ppermute | solution.py:279
  158.9 2.3 %collective-permute-start.12 = (bf16[384,768]{1,0:T(8,128)(2,1)S(1)}, bf16[384,768]{1,0:T(8,128)(2,1)S(1)}, u32[]{:S(2)}, u32[]{:S(2)}) collective-permute-start(bf16[384,768]{1,0:T(8,128)(2,1)S(1)} %get-tuple-element.77), channel_id=1, source_target_pairs={{0,64},{64,128},{128,192},{192,0},{1,65},{65,129},{129,193},{193,1... | collective-permute-start | bytes 1769480 | tf_op jit(solution)/shard_map/ppermute | solution.py:273
  161.3 2.7 %shard_map.137 = bf16[768,512]{1,0:T(8,128)(2,1)} custom-call(bf16[384,768]{1,0:T(8,128)(2,1)S(1)} %copy-done.8, bf16[384,512]{1,0:T(8,128)(2,1)S(1)} %copy-done.15, bf16[384,768]{1,0:T(8,128)(2,1)S(1)} %collective-permute-done.3.refs_2_, bf16[384,512]{1,0:T(8,128)(2,1)S(1)} %collective-permute-done.9.refs_3_, bf16[384,768]{1,0:T(8,128)(2,1)S(1)} %copy-done.4, ...), custom_call_target="tpu_custom_call" | custom-call | flops 12079595520 | bytes 4718592 | tf_op jit(solution)/shard_map/pallas_call | solution.py:41
  164.0 9.4 %collective-permute-done.12.g0 = bf16[384,768]{1,0:T(8,128)(2,1)S(1)} collective-permute-done((bf16[384,768]{1,0:T(8,128)(2,1)S(1)}, bf16[384,768]{1,0:T(8,128)(2,1)S(1)}, u32[]{:S(2)}, u32[]{:S(2)}) %collective-permute-start.12) | collective-permute-done | bytes 589856 | tf_op jit(solution)/shard_map/ppermute | solution.py:273
  173.4 3.4 %collective-permute-done.13.g1 = bf16[384,768]{1,0:T(8,128)(2,1)S(1)} collective-permute-done((bf16[384,768]{1,0:T(8,128)(2,1)S(1)}, bf16[384,768]{1,0:T(8,128)(2,1)S(1)}, u32[]{:S(2)}, u32[]{:S(2)}) %collective-permute-start.13) | collective-permute-done | bytes 589856 | tf_op jit(solution)/shard_map/ppermute | solution.py:279
  176.9 2.7 %shard_map.136 = (bf16[512,768]{1,0:T(8,128)(2,1)}, bf16[512,768]{1,0:T(8,128)(2,1)}) custom-call(bf16[512,384]{1,0:T(8,128)(2,1)S(1)} %get-tuple-element.73.x, bf16[384,768]{1,0:T(8,128)(2,1)S(1)} %collective-permute-done.12.g0, bf16[384,768]{1,0:T(8,128)(2,1)S(1)} %collective-permute-done.13.g1, f32[512,768]{1,0:T(8,128)S(1)} %get-tuple-element.79.pgate, ...), custom_call_target="tpu_custom_call" | custom-call | flops 6039797760 | bytes 6291456 | tf_op jit(solution)/shard_map/pallas_call | solution.py:41
  179.6 1.8 shard_map.134
  (59 shorter events, 9.5 us)
Async XLA Ops:
  4.1 52.2 %all-to-all-start.1 = ((bf16[64,24,512]{2,1,0:T(8,128)(2,1)}), bf16[64,24,512]{2,1,0:T(8,128)(2,1)S(1)}, u32[]{:S(2)}, u32[]{:S(2)}) async-start(bf16[64,24,512]{2,1,0:T(8,128)(2,1)} %bitcast.30), calls=%async_computation.1 | async-start | bytes 3145728 | tf_op jit(solution)/shard_map/all_to_all | solution.py:283
  56.3 5.7 %copy-start = (bf16[192,192]{1,0:T(8,128)(2,1)S(1)}, bf16[192,192]{1,0:T(8,128)(2,1)}, u32[]{:S(2)}) copy-start(bf16[192,192]{1,0:T(8,128)(2,1)} %constant.10.clone.packer_ref) | copy-start | bytes 221188
  56.3 45.7 %all-to-all-start = ((bf16[64,24,512]{2,1,0:T(8,128)(2,1)}), bf16[64,24,512]{2,1,0:T(8,128)(2,1)}, u32[]{:S(2)}, u32[]{:S(2)}) async-start(bf16[64,24,512]{2,1,0:T(8,128)(2,1)} %bitcast.29), calls=%async_computation | async-start | bytes 3145728 | tf_op jit(solution)/shard_map/all_to_all | solution.py:283
  62.7 1.2 copy-start.7
  64.6 11.0 %collective-permute-start.1 = (bf16[384,512]{1,0:T(8,128)(2,1)S(1)}, bf16[384,512]{1,0:T(8,128)(2,1)S(1)}, u32[]{:S(2)}, u32[]{:S(2)}) collective-permute-start(bf16[384,512]{1,0:T(8,128)(2,1)S(1)} %get-tuple-element.50), channel_id=1, source_target_pairs={{0,64},{64,128},{128,192},{192,0},{1,65},{65,129},{129,193},{193,1... | collective-permute-start | bytes 1179656 | tf_op jit(solution)/shard_map/ppermute | solution.py:273
  65.1 11.9 %collective-permute-start.2 = (bf16[384,512]{1,0:T(8,128)(2,1)S(1)}, bf16[384,512]{1,0:T(8,128)(2,1)S(1)}, u32[]{:S(2)}, u32[]{:S(2)}) collective-permute-start(bf16[384,512]{1,0:T(8,128)(2,1)S(1)} %get-tuple-element.51), channel_id=1, source_target_pairs={{0,192},{64,0},{128,64},{192,128},{1,193},{65,1},{129,65},{193,129... | collective-permute-start | bytes 1179656 | tf_op jit(solution)/shard_map/ppermute | solution.py:279
  77.8 24.2 %collective-permute-start.3 = (bf16[384,768]{1,0:T(8,128)(2,1)}, bf16[384,768]{1,0:T(8,128)(2,1)S(1)}, u32[]{:S(2)}, u32[]{:S(2)}) collective-permute-start(bf16[384,768]{1,0:T(8,128)(2,1)} %get-tuple-element.52.refs_0_), channel_id=1, source_target_pairs={{0,64},{64,128},{128,192},{192,0},{1,65},{65,129},{129,193},{193,1... | collective-permute-start | bytes 1769480 | tf_op jit(solution)/shard_map/ppermute | solution.py:273
  78.8 24.0 %collective-permute-start.4 = (bf16[384,768]{1,0:T(8,128)(2,1)}, bf16[384,768]{1,0:T(8,128)(2,1)S(1)}, u32[]{:S(2)}, u32[]{:S(2)}) collective-permute-start(bf16[384,768]{1,0:T(8,128)(2,1)} %get-tuple-element.52.refs_0_), channel_id=1, source_target_pairs={{0,192},{64,0},{128,64},{192,128},{1,193},{65,1},{129,65},{193,129... | collective-permute-start | bytes 1769480 | tf_op jit(solution)/shard_map/ppermute | solution.py:279
  79.8 22.2 %collective-permute-start = (bf16[384,512]{1,0:T(8,128)(2,1)S(1)}, bf16[384,512]{1,0:T(8,128)(2,1)S(1)}, u32[]{:S(2)}, u32[]{:S(2)}) collective-permute-start(bf16[384,512]{1,0:T(8,128)(2,1)S(1)} %get-tuple-element.47), channel_id=1, source_target_pairs={{0,128},{64,192},{128,0},{192,64},{1,129},{65,193},{129,1},{193,65... | collective-permute-start | bytes 1179656 | tf_op jit(solution)/shard_map/ppermute | solution.py:276
  102.0 10.3 %copy-start.16 = (bf16[384,512]{1,0:T(8,128)(2,1)}, bf16[384,512]{1,0:T(8,128)(2,1)S(1)}, u32[]{:S(2)}) copy-start(bf16[384,512]{1,0:T(8,128)(2,1)S(1)} %collective-permute-done.far_ref) | copy-start | bytes 1179652
  102.9 9.5 %copy-start.3 = (bf16[384,768]{1,0:T(8,128)(2,1)}, bf16[384,768]{1,0:T(8,128)(2,1)S(1)}, u32[]{:S(2)}) copy-start(bf16[384,768]{1,0:T(8,128)(2,1)S(1)} %collective-permute-done.4.refs_4_) | copy-start | bytes 1769476
  102.9 9.4 %collective-permute-start.5 = (bf16[192,768]{1,0:T(8,128)(2,1)S(1)}, bf16[192,768]{1,0:T(8,128)(2,1)S(1)}, u32[]{:S(2)}, u32[]{:S(2)}) collective-permute-start(bf16[192,768]{1,0:T(8,128)(2,1)S(1)} %slice.12), channel_id=1, source_target_pairs={{0,64},{64,128},{128,192},{192,0},{1,65},{65,129},{129,193},{193,1... | collective-permute-start | bytes 884744 | tf_op jit(solution)/shard_map/ppermute | solution.py:273
  103.4 9.0 %collective-permute-start.6 = (bf16[192,768]{1,0:T(8,128)(2,1)S(1)}, bf16[192,768]{1,0:T(8,128)(2,1)S(1)}, u32[]{:S(2)}, u32[]{:S(2)}) collective-permute-start(bf16[192,768]{1,0:T(8,128)(2,1)S(1)} %slice.13), channel_id=1, source_target_pairs={{0,192},{64,0},{128,64},{192,128},{1,193},{65,1},{129,65},{193,129... | collective-permute-start | bytes 884744 | tf_op jit(solution)/shard_map/ppermute | solution.py:279
  112.3 10.2 %copy-start.18 = (bf16[192,768]{1,0:T(8,128)(2,1)}, bf16[192,768]{1,0:T(8,128)(2,1)S(1)}, u32[]{:S(2)}) copy-start(bf16[192,768]{1,0:T(8,128)(2,1)S(1)} %collective-permute-done.5.refs_6_) | copy-start | bytes 884740
  112.3 10.2 %copy-start.20 = (bf16[192,768]{1,0:T(8,128)(2,1)}, bf16[192,768]{1,0:T(8,128)(2,1)S(1)}, u32[]{:S(2)}) copy-start(bf16[192,768]{1,0:T(8,128)(2,1)S(1)} %collective-permute-done.6.refs_7_) | copy-start | bytes 884740
  112.4 26.0 %collective-permute-start.7 = (bf16[2,384,768]{2,1,0:T(8,128)(2,1)}, bf16[2,384,768]{2,1,0:T(8,128)(2,1)}, u32[]{:S(2)}, u32[]{:S(2)}) collective-permute-start(bf16[2,384,768]{2,1,0:T(8,128)(2,1)} %get-tuple-element.60.g_ref.refs_1_), channel_id=1, source_target_pairs={{0,64},{64,128},{128,192},{192,0},{1,65},{65,129},{129,193},{193,1... | collective-permute-start | bytes 3538952 | tf_op jit(solution)/shard_map/ppermute | solution.py:273
  114.2 26.8 %collective-permute-start.8 = (bf16[2,384,768]{2,1,0:T(8,128)(2,1)}, bf16[2,384,768]{2,1,0:T(8,128)(2,1)}, u32[]{:S(2)}, u32[]{:S(2)}) collective-permute-start(bf16[2,384,768]{2,1,0:T(8,128)(2,1)} %get-tuple-element.60.g_ref.refs_1_), channel_id=1, source_target_pairs={{0,192},{64,0},{128,64},{192,128},{1,193},{65,1},{129,65},{193,129... | collective-permute-start | bytes 3538952 | tf_op jit(solution)/shard_map/ppermute | solution.py:279
  122.5 21.7 %copy-start.1 = (bf16[2,384,768]{2,1,0:T(8,128)(2,1)S(1)}, bf16[2,384,768]{2,1,0:T(8,128)(2,1)}, u32[]{:S(2)}) copy-start(bf16[2,384,768]{2,1,0:T(8,128)(2,1)} %get-tuple-element.60.g_ref.refs_1_) | copy-start | bytes 3538948
  122.5 57.0 %all-to-all-start.2 = ((bf16[64,8,1664]{2,1,0:T(8,128)(2,1)}), bf16[64,8,1664]{2,1,0:T(8,128)(2,1)S(1)}, u32[]{:S(2)}, u32[]{:S(2)}) async-start(bf16[64,8,1664]{2,1,0:T(8,128)(2,1)} %bitcast.28), calls=%async_computation.2 | async-start | bytes 3407872 | tf_op jit(solution)/shard_map/all_to_all | solution.py:283
  141.0 17.3 %collective-permute-start.10 = (bf16[384,512]{1,0:T(8,128)(2,1)}, bf16[384,512]{1,0:T(8,128)(2,1)S(1)}, u32[]{:S(2)}, u32[]{:S(2)}) collective-permute-start(bf16[384,512]{1,0:T(8,128)(2,1)} %get-tuple-element.75), channel_id=1, source_target_pairs={{0,192},{64,0},{128,64},{192,128},{1,193},{65,1},{129,65},{193,129... | collective-permute-start | bytes 1179656 | tf_op jit(solution)/shard_map/ppermute | solution.py:279
  141.0 17.3 %collective-permute-start.11 = (bf16[384,512]{1,0:T(8,128)(2,1)}, bf16[384,512]{1,0:T(8,128)(2,1)S(1)}, u32[]{:S(2)}, u32[]{:S(2)}) collective-permute-start(bf16[384,512]{1,0:T(8,128)(2,1)} %get-tuple-element.76), channel_id=1, source_target_pairs={{0,128},{64,192},{128,0},{192,64},{1,129},{65,193},{129,1},{193,65... | collective-permute-start | bytes 1179656 | tf_op jit(solution)/shard_map/ppermute | solution.py:276
  142.7 16.2 %collective-permute-start.9 = (bf16[384,512]{1,0:T(8,128)(2,1)}, bf16[384,512]{1,0:T(8,128)(2,1)S(1)}, u32[]{:S(2)}, u32[]{:S(2)}) collective-permute-start(bf16[384,512]{1,0:T(8,128)(2,1)} %get-tuple-element.74), channel_id=1, source_target_pairs={{0,64},{64,128},{128,192},{192,0},{1,65},{65,129},{129,193},{193,1... | collective-permute-start | bytes 1179656 | tf_op jit(solution)/shard_map/ppermute | solution.py:273
  152.5 8.8 %copy-start.4 = (bf16[384,768]{1,0:T(8,128)(2,1)S(1)}, bf16[384,768]{1,0:T(8,128)(2,1)}, u32[]{:S(2)}) copy-start(bf16[384,768]{1,0:T(8,128)(2,1)} %copy-done.3) | copy-start | bytes 1769476
  152.5 8.7 %copy-start.8 = (bf16[384,768]{1,0:T(8,128)(2,1)S(1)}, bf16[384,768]{1,0:T(8,128)(2,1)}, u32[]{:S(2)}) copy-start(bf16[384,768]{1,0:T(8,128)(2,1)} %get-tuple-element.52.refs_0_) | copy-start | bytes 1769476
  152.5 8.7 %copy-start.15 = (bf16[384,512]{1,0:T(8,128)(2,1)S(1)}, bf16[384,512]{1,0:T(8,128)(2,1)}, u32[]{:S(2)}) copy-start(bf16[384,512]{1,0:T(8,128)(2,1)} %get-tuple-element.83.refs_1_) | copy-start | bytes 1179652
  152.5 8.7 %copy-start.19 = (bf16[192,768]{1,0:T(8,128)(2,1)S(1)}, bf16[192,768]{1,0:T(8,128)(2,1)}, u32[]{:S(2)}) copy-start(bf16[192,768]{1,0:T(8,128)(2,1)} %copy-done.18) | copy-start | bytes 884740
  152.5 8.7 %copy-start.21 = (bf16[192,768]{1,0:T(8,128)(2,1)S(1)}, bf16[192,768]{1,0:T(8,128)(2,1)}, u32[]{:S(2)}) copy-start(bf16[192,768]{1,0:T(8,128)(2,1)} %copy-done.20) | copy-start | bytes 884740
  158.9 14.5 %collective-permute-start.12 = (bf16[384,768]{1,0:T(8,128)(2,1)S(1)}, bf16[384,768]{1,0:T(8,128)(2,1)S(1)}, u32[]{:S(2)}, u32[]{:S(2)}) collective-permute-start(bf16[384,768]{1,0:T(8,128)(2,1)S(1)} %get-tuple-element.77), channel_id=1, source_target_pairs={{0,64},{64,128},{128,192},{192,0},{1,65},{65,129},{129,193},{193,1... | collective-permute-start | bytes 1769480 | tf_op jit(solution)/shard_map/ppermute | solution.py:273
  161.2 15.6 %collective-permute-start.13 = (bf16[384,768]{1,0:T(8,128)(2,1)S(1)}, bf16[384,768]{1,0:T(8,128)(2,1)S(1)}, u32[]{:S(2)}, u32[]{:S(2)}) collective-permute-start(bf16[384,768]{1,0:T(8,128)(2,1)S(1)} %get-tuple-element.78), channel_id=1, source_target_pairs={{0,192},{64,0},{128,64},{192,128},{1,193},{65,1},{129,65},{193,129... | collective-permute-start | bytes 1769480 | tf_op jit(solution)/shard_map/ppermute | solution.py:279
  176.9 2.7 %copy-start.2 = (bf16[192,192]{1,0:T(8,128)(2,1)S(1)}, bf16[192,192]{1,0:T(8,128)(2,1)}, u32[]{:S(2)}) copy-start(bf16[192,192]{1,0:T(8,128)(2,1)} %constant.11.clone.liner_ref) | copy-start | bytes 221188
  176.9 2.7 %copy-start.5 = (s32[128,2]{0,1:T(2,128)S(1)}, s32[128,2]{0,1:T(2,128)}, u32[]{:S(2)}) copy-start(s32[128,2]{0,1:T(2,128)} %param.10) | copy-start | bytes 3076
  176.9 2.7 %copy-start.6 = (bf16[128,2]{0,1:T(2,128)(2,1)S(1)}, bf16[128,2]{0,1:T(2,128)(2,1)}, u32[]{:S(2)}) copy-start(bf16[128,2]{0,1:T(2,128)(2,1)} %param.11) | copy-start | bytes 1540
  (7 other events, 6.2 us)
